TPU v7x, 256 devices: a whole 4x4x8 slice. The times are simulated.
256 devices in a mesh: dp: 2 (over x_hi), fsdp: 2 (over core), tensor: 64 (over z, y, x_lo).
Axes of the slice: x: 4 (x_hi: 2, x_lo: 2; x = x_hi * 2 + x_lo), y: 4, z: 8, core: 2. Of those that a mesh axis runs over, the one named last changes fastest.
Arguments:
- weight: float32 [4096, 8192], P('fsdp', 'tensor'), may hold values from -6 to 6
- momentum: float32 [4096, 8192], P('fsdp', 'tensor'), may hold values from -180 to 180
- right_basis: float32 [256, 8192], P('fsdp', 'tensor'), may hold values from -0.0625 to 0.0625
- gradients: bfloat16 [1, 2, 4096, 8192], P(None, 'dp', 'fsdp', 'tensor'), may hold values from -6 to 6
Outputs:
- new_weight: float32 [4096, 8192], P('fsdp', 'tensor')
- new_momentum: float32 [4096, 8192], P('fsdp', 'tensor')
- new_basis: float32 [256, 8192], P('fsdp', 'tensor')
All inputs are finite; a program needn't handle non-finite values.
Results may differ from a plain program's by a relative error of at most 0.0003.
Values sent between devices are 32-bit elements; how exact they have to be, the bound alone decides.
No kernel may reach another device: no remote copies, remote signals or barrier semaphores. Data moves between devices by JAX's collectives and lax.ppermute only.
A program may use at most 64 MiB of HBM per device.

v0:
```python
import math

import jax
import jax.numpy as jnp
from jax import lax
from jax.experimental import pallas as pl
from jax.experimental.pallas import tpu as pltpu
from jax.sharding import Mesh
from jax.sharding import PartitionSpec as P

D = 8192
ROWS = 4096
RANK = 256


highest = lax.Precision.HIGHEST
step_size = 0.3
drop_share = 0.05
guard_term = 1e-06

PLANE = ("dp", "y", "xl")
TENSOR = ("z", "y", "xl")


def contract(left, right, left_dim, right_dim):
    return lax.dot_general(
        left,
        right,
        (((left_dim,), (right_dim,)), ((), ())),
        precision=highest,
        preferred_element_type=jnp.float32,
    )


def in_hbm(value):
    return pltpu.with_memory_space_constraint(value, pltpu.HBM)


def swapped(value, axis):
    return lax.ppermute(value, axis, [(0, 1), (1, 0)])


def sent_to_all(value, axis):
    length = lax.axis_size(axis)
    return lax.all_to_all(
        jnp.broadcast_to(value[None], (length, *value.shape)), axis, 0, 0, tiled=True
    )


def sum_at_owner(value, axis):
    length = lax.axis_size(axis)
    pieces = value.reshape(length, len(value) // length, *value.shape[1:])
    return lax.all_to_all(pieces, axis, 0, 0, tiled=True).sum(axis=0)


def gather(value, axis):
    pieces = sent_to_all(value, axis)
    return pieces.reshape(-1, *value.shape[1:])


KERNEL_VMEM = 16 * 2**20
BLOCK = 64
TILE = 8


def block_inverse(block):
    size = len(block)
    rows = lax.broadcasted_iota(jnp.int32, (size, size), 0)
    columns = lax.broadcasted_iota(jnp.int32, (size, size), 1)
    identity = (rows == columns).astype(jnp.float32)
    both = jnp.concatenate([block, identity], axis=1)
    tiles = [both[TILE * t : TILE * t + TILE] for t in range(size // TILE)]
    in_tile = lax.broadcasted_iota(jnp.int32, (TILE, 1), 0)
    for k in range(size - 1):
        t, s = divmod(k, TILE)
        row = tiles[t][s : s + 1]
        scaled = row * (1.0 / row[:, k : k + 1])
        for u in range(t, size // TILE):
            column = tiles[u][:, k : k + 1]
            if u == t:
                if s == TILE - 1:
                    continue
                column = jnp.where(in_tile > s, column, 0.0)
            tiles[u] = tiles[u] - column * scaled
    both = jnp.concatenate(tiles, axis=0)
    pivots = jnp.sum(jnp.where(rows == columns, both[:, :size], 0.0), axis=1, keepdims=True)
    return both[:, size:] * lax.rsqrt(pivots)


def split(value):
    high = value.astype(jnp.bfloat16)
    return high, (value - high.astype(jnp.float32)).astype(jnp.bfloat16)


def three_pass(left, right, left_dim, right_dim):
    def product(a, b):
        return lax.dot_general(
            a, b, (((left_dim,), (right_dim,)), ((), ())), preferred_element_type=jnp.float32
        )

    left_high, left_low = split(left)
    right_high, right_low = split(right)
    return product(left_high, right_high) + (
        product(left_high, right_low) + product(left_low, right_high)
    )


def moments_kernel(sketch_ref, momentum_ref, own_ref, other_ref, gram_ref, product_ref, total_ref):
    @pl.when(pl.program_id(0) == 0)
    def _():
        gram_ref[...] = jnp.zeros_like(gram_ref)
        product_ref[...] = jnp.zeros_like(product_ref)

    sketch = sketch_ref[...]
    total = momentum_ref[...] + (own_ref[...].astype(jnp.float32) + other_ref[...])
    total_ref[...] = total
    gram_ref[...] += contract(sketch, sketch, 0, 0)
    product_ref[...] += three_pass(sketch, total, 0, 0)


def moments(sketch, momentum, own, other):
    rows, columns = momentum.shape
    step = rows // 4

    def by_rows(width):
        return pl.BlockSpec((step, width), lambda i: (i, 0))

    def whole(*shape):
        return pl.BlockSpec(shape, lambda i: (0, 0))

    return pl.pallas_call(
        moments_kernel,
        compiler_params=pltpu.CompilerParams(vmem_limit_bytes=KERNEL_VMEM),
        grid=(rows // step,),
        out_shape=(
            jax.ShapeDtypeStruct((RANK, RANK), jnp.float32),
            jax.ShapeDtypeStruct((RANK, columns), jnp.float32),
            pltpu.HBM((rows, columns), jnp.float32),
        ),
        in_specs=[by_rows(RANK), by_rows(columns), by_rows(columns), by_rows(columns)],
        out_specs=(whole(RANK, RANK), whole(RANK, columns), by_rows(columns)),
    )(sketch, in_hbm(momentum), in_hbm(own), other)


def coefficients_kernel(
    gram_ref, other_gram_ref, product_ref, other_product_ref,
    inverse_ref, coefficients_ref, squares_ref, held,
):
    held[...] = gram_ref[...] + other_gram_ref[...]
    for first in range(0, RANK, BLOCK):
        last = first + BLOCK
        inverse = block_inverse(held[first:last, first:last])
        lane = lax.broadcasted_iota(jnp.int32, (BLOCK, RANK), 1)
        row = lax.broadcasted_iota(jnp.int32, (BLOCK, RANK), 0)
        inside = (lane >= first) & (lane < last)
        panel = jnp.where(inside, (lane - first == row).astype(jnp.float32), held[first:last, :])
        panel = contract(inverse, panel, 1, 0)
        held[first:last, :] = panel
        if last < RANK:
            rest = held[last:, :]
            factor = contract(rest[:, first:last], inverse, 1, 1)
            lane = lax.broadcasted_iota(jnp.int32, (RANK - last, RANK), 1)
            inside = (lane >= first) & (lane < last)
            held[last:, :] = jnp.where(inside, 0.0, rest) - contract(factor, panel, 1, 0)
    row = lax.broadcasted_iota(jnp.int32, (RANK, RANK), 0)
    lane = lax.broadcasted_iota(jnp.int32, (RANK, RANK), 1)
    inverse = jnp.where(lane <= row, held[...], 0.0)
    coefficients = contract(inverse, product_ref[...] + other_product_ref[...], 1, 0)
    coefficients_ref[...] = coefficients
    inverse_ref[...] = inverse.T
    ones = jnp.ones((8, coefficients.shape[1]), jnp.float32)
    squares = contract(ones, coefficients * coefficients, 1, 1)
    squares_ref[...] = jnp.broadcast_to(squares[None, :1], squares_ref.shape)


def small_part(gram, other_gram, product, other_product, copies):
    def whole(shape):
        return pl.BlockSpec(shape, lambda i: (0,) * len(shape))

    return pl.pallas_call(
        coefficients_kernel,
        compiler_params=pltpu.CompilerParams(vmem_limit_bytes=KERNEL_VMEM),
        out_shape=(
            pltpu.HBM(gram.shape, jnp.float32),
            pltpu.HBM(product.shape, jnp.float32),
            jax.ShapeDtypeStruct((copies, 1, RANK), jnp.float32),
        ),
        in_specs=[pl.BlockSpec(memory_space=pltpu.VMEM)] * 4,
        grid=(1,),
        out_specs=(whole(gram.shape), whole(product.shape), whole((copies, 1, RANK))),
        scratch_shapes=[pltpu.VMEM((RANK, RANK), jnp.float32)],
    )(gram, other_gram, product, other_product)


def update_kernel(
    first_ref, squares_ref, sketch_ref, inverse_ref, coefficients_ref, weight_ref, total_ref,
    weight_out_ref, momentum_out_ref, basis_ref, change_ref,
):
    columns = weight_ref.shape[1]

    @pl.when(pl.program_id(0) == 0)
    def _():
        step_scale = step_size * math.sqrt(ROWS * D / RANK)
        scale = lax.rsqrt(jnp.sum(squares_ref[:, 0, :], axis=0, keepdims=True) + guard_term)
        inverse = inverse_ref[...]
        coefficients = coefficients_ref[...]
        change_ref[:, :columns] = step_scale * contract(inverse * scale, coefficients, 1, 0)
        change_ref[:, columns:] = drop_share * contract(inverse, coefficients, 1, 0)
        share = basis_ref.shape[0]
        row = lax.broadcasted_iota(jnp.int32, (share, RANK), 0) + first_ref[0]
        lane = lax.broadcasted_iota(jnp.int32, (share, RANK), 1)
        column = jnp.sum(jnp.where(row == lane, scale, 0.0), axis=1, keepdims=True)
        first = pl.multiple_of(first_ref[0], share)
        basis_ref[...] = coefficients_ref[pl.ds(first, share), :] * column

    change = three_pass(sketch_ref[...], change_ref[...], 1, 0)
    weight_out_ref[...] = weight_ref[...] - change[:, :columns]
    momentum_out_ref[...] = total_ref[...] - change[:, columns:]


def updates(first, squares, sketch, inverse, coefficients, weight, total, share):
    rows, columns = weight.shape
    step = rows // 4

    def whole(array):
        return pl.BlockSpec(array.shape, lambda i, first: (0,) * array.ndim)

    def by_rows(width):
        return pl.BlockSpec((step, width), lambda i, first: (i, 0))

    return pl.pallas_call(
        update_kernel,
        compiler_params=pltpu.CompilerParams(vmem_limit_bytes=KERNEL_VMEM),
        grid_spec=pltpu.PrefetchScalarGridSpec(
            num_scalar_prefetch=1,
            grid=(rows // step,),
            in_specs=[
                whole(squares),
                by_rows(RANK),
                whole(inverse),
                whole(coefficients),
                by_rows(columns),
                by_rows(columns),
            ],
            out_specs=(
                by_rows(columns),
                by_rows(columns),
                pl.BlockSpec((share, columns), lambda i, first: (0, 0)),
            ),
            scratch_shapes=[pltpu.VMEM((RANK, 2 * columns), jnp.float32)],
        ),
        out_shape=(
            jax.ShapeDtypeStruct(weight.shape, jnp.float32),
            jax.ShapeDtypeStruct(weight.shape, jnp.float32),
            jax.ShapeDtypeStruct((share, columns), jnp.float32),
        ),
    )(
        first, squares, sketch, in_hbm(inverse), in_hbm(coefficients), in_hbm(weight), in_hbm(total)
    )


def split_in_three(value):
    high, _ = split(value)
    middle = value - high.astype(jnp.float32)
    middle_part = middle.astype(jnp.bfloat16)
    return high, middle_part, (middle - middle_part.astype(jnp.float32)).astype(jnp.bfloat16)


def term_kernel(core_ref, momentum_ref, gradient_ref, own_ref, other_ref, term_ref, wide_ref):
    gradient = gradient_ref[...].astype(jnp.float32)
    wide_ref[...] = gradient
    a1, a2, a3 = split_in_three(0.5 * momentum_ref[...] + gradient)
    left, right = jnp.concatenate([a1, a2], axis=1), jnp.concatenate([a1, a3], axis=1)

    def product(a, b):
        return lax.dot_general(
            a, b, (((1,), (1,)), ((), ())), preferred_element_type=jnp.float32
        )

    halves = []
    for half in range(2):
        basis = jnp.where(core_ref[0] == half, own_ref[...], other_ref[...])
        b1, b2, b3 = split_in_three(basis)
        halves.append(
            product(left, jnp.concatenate([b1, b1], axis=1))
            + (
                product(left, jnp.concatenate([b2, b2], axis=1))
                + product(right, jnp.concatenate([b3, b1], axis=1))
            )
        )
    term_ref[...] = jnp.concatenate(halves, axis=1)


def sketch_term(core, momentum, gradient, own, other):
    rows, columns = momentum.shape
    step = rows // 4

    def by_rows(width):
        return pl.BlockSpec((step, width), lambda i, core: (i, 0))

    def whole(array):
        return pl.BlockSpec(array.shape, lambda i, core: (0, 0))

    return pl.pallas_call(
        term_kernel,
        compiler_params=pltpu.CompilerParams(vmem_limit_bytes=KERNEL_VMEM),
        grid_spec=pltpu.PrefetchScalarGridSpec(
            num_scalar_prefetch=1,
            grid=(rows // step,),
            in_specs=[by_rows(columns), by_rows(columns), whole(own), whole(other)],
            out_specs=(by_rows(RANK), by_rows(columns)),
        ),
        out_shape=(
            jax.ShapeDtypeStruct((rows, RANK), jnp.float32),
            jax.ShapeDtypeStruct((rows, columns), jnp.float32),
        ),
    )(core, in_hbm(momentum), in_hbm(gradient), in_hbm(own), other)


def step(weight, momentum, right_basis, gradients):
    share = len(right_basis)
    core = jnp.reshape(lax.axis_index("fsdp"), (1,)).astype(jnp.int32)
    own = gradients[0, 0]
    term, gradient = sketch_term(core, momentum, own, right_basis, swapped(right_basis, "fsdp"))
    sketch = sum_at_owner(term, PLANE)
    gradient, sketch = lax.optimization_barrier((gradient, sketch))
    other = swapped(gradient, "dp")
    sketch = sum_at_owner(sketch, "z")
    sketch = gather(sketch, "z")
    other, sketch = lax.optimization_barrier((other, sketch))
    sketch = gather(sketch, PLANE)

    gram, product, total = moments(sketch, momentum, own, other)
    inverse, coefficients, squares = small_part(
        gram, swapped(gram, "fsdp"), product, swapped(product, "fsdp"), lax.axis_size(TENSOR)
    )
    squares = lax.all_to_all(squares, TENSOR, 0, 0, tiled=True)
    weight, momentum, right_basis = updates(
        core * share, squares, sketch, inverse, coefficients, weight, total, share
    )
    return weight, momentum, right_basis


def solution(mesh):
    fine = Mesh(mesh.devices.reshape(2, 2, 8, 4, 2), ("dp", "fsdp", "z", "y", "xl"))
    placed = P("fsdp", TENSOR)
    return jax.shard_map(
        step,
        mesh=fine,
        in_specs=(placed, placed, placed, P(None, "dp", "fsdp", TENSOR)),
        out_specs=(placed, placed, placed),
        check_vma=False,
    )
```

profile of v0, /device:TPU:1, one launch (start us, length us, event | category | flops | bytes accessed | tf_op | source)
XLA Modules:
  0.0 156.0 jit_solution(11857169941047601952)
XLA Ops:
  0.6 3.3 %collective-permute-start = (f32[128,128]{1,0:T(8,128)}, f32[128,128]{1,0:T(8,128)S(1)}, u32[]{:S(2)}, u32[]{:S(2)}) collective-permute-start(f32[128,128]{1,0:T(8,128)} %own_ref.1), channel_id=1, source_target_pairs={{0,64},{64,0},{1,65},{65,1},{2,66},{66,2},{3,67},{67,3},{4,68},{68... | collective-permute-start | bytes 196616 | tf_op jit(solution)/shard_map/ppermute | solution.py:40
  3.9 1.1 collective-permute-done.other_ref
  5.0 3.8 %shard_map.67 = (f32[2048,256]{1,0:T(8,128)S(1)}, f32[2048,128]{1,0:T(8,128)S(1)}) custom-call(s32[1]{0:T(128)} %bitcast.core_ref, f32[2048,128]{1,0:T(8,128)} %momentum_ref.3, bf16[2048,128]{1,0:T(8,128)(2,1)} %bitcast.9, f32[128,128]{1,0:T(8,128)} %own_ref.1, f32[128,128]{1,0:T(8,128)S(1)} %collective-permute-done.other_ref), custom_call_target="tpu_custom_call" | custom-call | tf_op jit(solution)/shard_map/pallas_call | solution.py:304
  8.8 32.4 %all_to_all.25 = f32[16,128,256]{2,1,0:T(8,128)S(1)} all-to-all(f32[16,128,256]{2,1,0:T(8,128)S(1)} %bitcast.8), channel_id=1, replica_groups=mesh['dp'=2,'fsdp'=2,'z'=8,'y'=4,'xl'=2] {'dp','y','xl'}, dimensions={0} | all-to-all | bytes 4194304 | tf_op jit(solution)/shard_map/all_to_all | solution.py:53
  41.3 0.1 reduce_sum.18
  41.4 0.4 collective-permute-start.1
  41.9 15.9 %all_to_all.26 = f32[8,16,256]{2,1,0:T(8,128)S(1)} all-to-all(f32[8,16,256]{2,1,0:T(8,128)S(1)} %bitcast.11), channel_id=1, replica_groups=mesh['dp'=2,'fsdp'=2,'z'=8,'y'=4,'xl'=2] {'z'}, dimensions={0} | all-to-all | bytes 262144 | tf_op jit(solution)/shard_map/all_to_all | solution.py:53
  57.8 10.3 %all_to_all.27 = f32[8,16,256]{2,1,0:T(8,128)S(1)} all-to-all(f32[8,16,256]{2,1,0:T(8,128)S(1)} %broadcast_in_dim.4), channel_id=1, replica_groups=mesh['dp'=2,'fsdp'=2,'z'=8,'y'=4,'xl'=2] {'z'}, dimensions={0} | all-to-all | bytes 262144 | tf_op jit(solution)/shard_map/all_to_all | solution.py:45
  68.1 0.0 collective-permute-done.1.other_ref
  68.1 0.2 broadcast_in_dim.5
  68.3 29.3 %all_to_all.28 = f32[16,128,256]{2,1,0:T(8,128)S(1)} all-to-all(f32[16,128,256]{2,1,0:T(8,128)S(1)} %broadcast_in_dim.5), channel_id=1, replica_groups=mesh['dp'=2,'fsdp'=2,'z'=8,'y'=4,'xl'=2] {'dp','y','xl'}, dimensions={0} | all-to-all | bytes 4194304 | tf_op jit(solution)/shard_map/all_to_all | solution.py:45
  97.6 4.9 %shard_map.68 = (f32[256,256]{1,0:T(8,128)S(1)}, f32[256,128]{1,0:T(8,128)S(1)}, f32[2048,128]{1,0:T(8,128)}) custom-call(f32[2048,256]{1,0:T(8,128)S(1)} %bitcast.6, f32[2048,128]{1,0:T(8,128)} %momentum_ref.3, bf16[2048,128]{1,0:T(8,128)(2,1)} %bitcast.10, f32[2048,128]{1,0:T(8,128)S(1)} %collective-permute-done.1.other_ref), custom_call_target="tpu_custom_call" | custom-call | tf_op jit(solution)/shard_map/pallas_call | solution.py:131
  102.5 5.2 %collective-permute-start.2 = (f32[256,256]{1,0:T(8,128)S(1)}, f32[256,256]{1,0:T(8,128)S(1)}, u32[]{:S(2)}, u32[]{:S(2)}) collective-permute-start(f32[256,256]{1,0:T(8,128)S(1)} %get-tuple-element.21.gram_ref), channel_id=1, source_target_pairs={{0,64},{64,0},{1,65},{65,1},{2,66},{66,2},{3,67},{67,3},{4,68},{68... | collective-permute-start | bytes 786440 | tf_op jit(solution)/shard_map/ppermute | solution.py:40
  107.7 0.0 collective-permute-start.3
  107.7 1.3 collective-permute-done.3.other_product_ref
  109.1 0.0 collective-permute-done.2.other_gram_ref
  109.1 25.0 %shard_map.69 = (f32[256,256]{1,0:T(8,128)}, f32[256,128]{1,0:T(8,128)}, f32[64,1,256]{2,1,0:T(1,128)}) custom-call(f32[256,256]{1,0:T(8,128)S(1)} %get-tuple-element.21.gram_ref, f32[256,256]{1,0:T(8,128)S(1)} %collective-permute-done.2.other_gram_ref, f32[256,128]{1,0:T(8,128)S(1)} %get-tuple-element.22.product_ref, ...), custom_call_target="tpu_custom_call" | custom-call | tf_op jit(solution)/shard_map/pallas_call | solution.py:180
  134.0 7.2 %all-to-all-start.4 = ((f32[64,1,256]{2,1,0:T(1,128)}), f32[64,1,256]{2,1,0:T(1,128)S(1)}, u32[]{:S(2)}, u32[]{:S(2)}) async-start(f32[64,1,256]{2,1,0:T(1,128)} %get-tuple-element.23), calls=%async_computation.4 | async-start | bytes 131072 | tf_op jit(solution)/shard_map/all_to_all | solution.py:337
  141.2 9.6 %all-to-all-done.4.squares_ref = f32[64,1,256]{2,1,0:T(1,128)S(1)} async-done(((f32[64,1,256]{2,1,0:T(1,128)}), f32[64,1,256]{2,1,0:T(1,128)S(1)}, u32[]{:S(2)}, u32[]{:S(2)}) %all-to-all-start.4) | async-done | bytes 65568 | tf_op jit(solution)/shard_map/all_to_all | solution.py:337
  150.8 5.2 %shard_map.70 = (f32[2048,128]{1,0:T(8,128)}, f32[2048,128]{1,0:T(8,128)}, f32[128,128]{1,0:T(8,128)}) custom-call(s32[1]{0:T(128)S(6)} %mul.3.first_ref, f32[64,1,256]{2,1,0:T(1,128)S(1)} %all-to-all-done.4.squares_ref, f32[2048,256]{1,0:T(8,128)S(1)} %bitcast.7, f32[256,256]{1,0:T(8,128)} %get-tuple-element.24.inverse_ref, ...), custom_call_target="tpu_custom_call" | custom-call | tf_op jit(solution)/shard_map/pallas_call | solution.py:231
  (2 shorter events, 0.0 us)
Async XLA Ops:
  0.6 4.4 %collective-permute-start = (f32[128,128]{1,0:T(8,128)}, f32[128,128]{1,0:T(8,128)S(1)}, u32[]{:S(2)}, u32[]{:S(2)}) collective-permute-start(f32[128,128]{1,0:T(8,128)} %own_ref.1), channel_id=1, source_target_pairs={{0,64},{64,0},{1,65},{65,1},{2,66},{66,2},{3,67},{67,3},{4,68},{68... | collective-permute-start | bytes 196616 | tf_op jit(solution)/shard_map/ppermute | solution.py:40
  41.4 26.7 %collective-permute-start.1 = (f32[2048,128]{1,0:T(8,128)S(1)}, f32[2048,128]{1,0:T(8,128)S(1)}, u32[]{:S(2)}, u32[]{:S(2)}) collective-permute-start(f32[2048,128]{1,0:T(8,128)S(1)} %get-tuple-element.17), channel_id=1, source_target_pairs={{0,128},{128,0},{1,129},{129,1},{2,130},{130,2},{3,131},{131,3},{4... | collective-permute-start | bytes 3145736 | tf_op jit(solution)/shard_map/ppermute | solution.py:40
  102.5 6.6 %collective-permute-start.2 = (f32[256,256]{1,0:T(8,128)S(1)}, f32[256,256]{1,0:T(8,128)S(1)}, u32[]{:S(2)}, u32[]{:S(2)}) collective-permute-start(f32[256,256]{1,0:T(8,128)S(1)} %get-tuple-element.21.gram_ref), channel_id=1, source_target_pairs={{0,64},{64,0},{1,65},{65,1},{2,66},{66,2},{3,67},{67,3},{4,68},{68... | collective-permute-start | bytes 786440 | tf_op jit(solution)/shard_map/ppermute | solution.py:40
  107.7 1.3 collective-permute-start.3
  134.0 16.8 %all-to-all-start.4 = ((f32[64,1,256]{2,1,0:T(1,128)}), f32[64,1,256]{2,1,0:T(1,128)S(1)}, u32[]{:S(2)}, u32[]{:S(2)}) async-start(f32[64,1,256]{2,1,0:T(1,128)} %get-tuple-element.23), calls=%async_computation.4 | async-start | bytes 131072 | tf_op jit(solution)/shard_map/all_to_all | solution.py:337
where the time goes:
time: 156 us
  blocking collectives  87.9 us (56%)
  Pallas kernels  38.9 us (25%)
  starting transfers between devices  16.1 us (10%)
  waiting for transfers between devices  12 us (8%)
    all_to_all x2, blocking collectives, sum_at_owner(): return lax.all_to_all(pieces, axis, 0, 0, tiled=True).sum(axis=0)  48.3 us
    all_to_all x2, blocking collectives, sent_to_all(): lax.all_to_all(jnp.broadcast_to(value[None], (length, *value.shape)), axi...  39.6 us
    pallas_call x1, Pallas kernels, small_part(): pl.pallas_call(coefficients_kernel, compiler_params=pltpu.CompilerParams(...  25 us
    all_to_all x1, waiting for transfers between devices, step(): squares = lax.all_to_all(squares, TENSOR, 0, 0, tiled=True)  9.59 us
    ppermute x4, starting transfers between devices, swapped(): return lax.ppermute(value, axis, [(0, 1), (1, 0)])  8.95 us
    all_to_all x1, starting transfers between devices, step(): squares = lax.all_to_all(squares, TENSOR, 0, 0, tiled=True)  7.18 us
    pallas_call x1, Pallas kernels, updates(): pl.pallas_call(update_kernel, compiler_params=pltpu.CompilerParams(vmem_l...  5.18 us
    pallas_call x1, Pallas kernels, moments(): pl.pallas_call(moments_kernel, compiler_params=pltpu.CompilerParams(vmem_...  4.93 us
  transfers between devices with their start and end apart: 5, of which 3 were waited for; matrix products, arithmetic and copies ran while one was open for 0% of the time, Pallas kernels for 0%

commit v1 on v0

--- a/solution.py
+++ b/solution.py
@@ -18,8 +18,8 @@
 drop_share = 0.05
 guard_term = 1e-06
 
-PLANE = ("dp", "y", "xl")
-TENSOR = ("z", "y", "xl")
+NEAR = ("dp", "zl", "y", "xl")
+TENSOR = ("zh", "zl", "y", "xl")
 
 
 def contract(left, right, left_dim, right_dim):
@@ -65,26 +65,62 @@
 
 def block_inverse(block):
     size = len(block)
+    width = 2 * size
     rows = lax.broadcasted_iota(jnp.int32, (size, size), 0)
     columns = lax.broadcasted_iota(jnp.int32, (size, size), 1)
-    identity = (rows == columns).astype(jnp.float32)
-    both = jnp.concatenate([block, identity], axis=1)
-    tiles = [both[TILE * t : TILE * t + TILE] for t in range(size // TILE)]
-    in_tile = lax.broadcasted_iota(jnp.int32, (TILE, 1), 0)
-    for k in range(size - 1):
-        t, s = divmod(k, TILE)
-        row = tiles[t][s : s + 1]
-        scaled = row * (1.0 / row[:, k : k + 1])
-        for u in range(t, size // TILE):
-            column = tiles[u][:, k : k + 1]
-            if u == t:
-                if s == TILE - 1:
-                    continue
-                column = jnp.where(in_tile > s, column, 0.0)
-            tiles[u] = tiles[u] - column * scaled
-    both = jnp.concatenate(tiles, axis=0)
-    pivots = jnp.sum(jnp.where(rows == columns, both[:, :size], 0.0), axis=1, keepdims=True)
-    return both[:, size:] * lax.rsqrt(pivots)
+    both = jnp.concatenate([block, (rows == columns).astype(jnp.float32)], axis=1)
+    tiles = [both[first : first + TILE] for first in range(0, size, TILE)]
+    place = lax.broadcasted_iota(jnp.int32, (TILE, width), 0)
+
+    def column(value, k):
+        return jnp.broadcast_to(value[:, k : k + 1], (TILE, width))
+
+    def row(value, k):
+        return jnp.broadcast_to(value[k : k + 1, :], (TILE, width))
+
+    def stacked(values):
+        result = values[0]
+        for k in range(1, TILE):
+            result = jnp.where(place == k, values[k], result)
+        return result
+
+    finished = []
+    for t, tile in enumerate(tiles):
+        entry, factor, reciprocal, inverse = {}, {}, {}, {}
+        for j in range(TILE):
+            spread = column(tile, TILE * t + j)
+            for i in range(j, TILE):
+                entry[i, j] = row(spread, i)
+        for j in range(TILE):
+            reciprocal[j] = 1.0 / entry[j, j]
+            for i in range(j + 1, TILE):
+                factor[i, j] = entry[i, j] * reciprocal[j]
+                for k in range(j + 1, i + 1):
+                    entry[i, k] = entry[i, k] - factor[i, j] * entry[k, j]
+        for j in range(TILE):
+            for i in range(j + 1, TILE):
+                total = factor[i, j]
+                for k in range(j + 1, i):
+                    total = total + factor[i, k] * inverse[k, j]
+                inverse[i, j] = -total
+        old = [row(tile, i) for i in range(TILE)]
+        new = []
+        for i in range(TILE):
+            total = old[i]
+            for j in range(i):
+                total = total + inverse[i, j] * old[j]
+            new.append(total)
+        finished.append(stacked(new) * lax.rsqrt(stacked([entry[j, j] for j in range(TILE)])))
+        for u in range(t + 1, size // TILE):
+            spread = [column(tiles[u], TILE * t + j) for j in range(TILE)]
+            rest = tiles[u]
+            for j in range(TILE):
+                total = spread[j]
+                for k in range(j):
+                    total = total + inverse[j, k] * spread[k]
+                rest = rest - (total * reciprocal[j]) * new[j]
+            tiles[u] = rest
+    return jnp.concatenate(finished, axis=0)[:, size:]
 
 
 def split(value):
@@ -105,41 +141,61 @@
     )
 
 
-def moments_kernel(sketch_ref, momentum_ref, own_ref, other_ref, gram_ref, product_ref, total_ref):
-    @pl.when(pl.program_id(0) == 0)
+def moments_kernel(
+    replica_ref, sketch_ref, momentum_ref, own_ref, near_ref, far_ref,
+    gram_ref, product_ref, total_ref,
+):
+    step = pl.program_id(0)
+
+    @pl.when(step == 0)
     def _():
         gram_ref[...] = jnp.zeros_like(gram_ref)
         product_ref[...] = jnp.zeros_like(product_ref)
 
     sketch = sketch_ref[...]
-    total = momentum_ref[...] + (own_ref[...].astype(jnp.float32) + other_ref[...])
+    in_own_half = step // (pl.num_programs(0) // 2) == replica_ref[0]
+    other = jnp.where(in_own_half, near_ref[...], far_ref[...])
+    total = momentum_ref[...] + (own_ref[...].astype(jnp.float32) + other)
     total_ref[...] = total
     gram_ref[...] += contract(sketch, sketch, 0, 0)
     product_ref[...] += three_pass(sketch, total, 0, 0)
 
 
-def moments(sketch, momentum, own, other):
+def moments(replica, sketch, momentum, own, near, far):
     rows, columns = momentum.shape
-    step = rows // 4
+    steps = 4
+    step = rows // steps
 
     def by_rows(width):
-        return pl.BlockSpec((step, width), lambda i: (i, 0))
+        return pl.BlockSpec((step, width), lambda i, replica: (i, 0))
+
+    def by_half(width):
+        return pl.BlockSpec((step, width), lambda i, replica: (i % (steps // 2), 0))
 
     def whole(*shape):
-        return pl.BlockSpec(shape, lambda i: (0, 0))
+        return pl.BlockSpec(shape, lambda i, replica: (0, 0))
 
     return pl.pallas_call(
         moments_kernel,
         compiler_params=pltpu.CompilerParams(vmem_limit_bytes=KERNEL_VMEM),
-        grid=(rows // step,),
+        grid_spec=pltpu.PrefetchScalarGridSpec(
+            num_scalar_prefetch=1,
+            grid=(steps,),
+            in_specs=[
+                by_rows(RANK),
+                by_rows(columns),
+                by_rows(columns),
+                by_half(columns),
+                by_half(columns),
+            ],
+            out_specs=(whole(RANK, RANK), whole(RANK, columns), by_rows(columns)),
+        ),
         out_shape=(
             jax.ShapeDtypeStruct((RANK, RANK), jnp.float32),
             jax.ShapeDtypeStruct((RANK, columns), jnp.float32),
             pltpu.HBM((rows, columns), jnp.float32),
         ),
-        in_specs=[by_rows(RANK), by_rows(columns), by_rows(columns), by_rows(columns)],
-        out_specs=(whole(RANK, RANK), whole(RANK, columns), by_rows(columns)),
-    )(sketch, in_hbm(momentum), in_hbm(own), other)
+    )(replica, sketch, in_hbm(momentum), in_hbm(own), near, far)
 
 
 def coefficients_kernel(
@@ -266,10 +322,12 @@
     return high, middle_part, (middle - middle_part.astype(jnp.float32)).astype(jnp.bfloat16)
 
 
-def term_kernel(core_ref, momentum_ref, gradient_ref, own_ref, other_ref, term_ref, wide_ref):
+def term_kernel(
+    place_ref, momentum_ref, gradient_ref, near_ref, own_ref, other_ref, term_ref, wide_ref
+):
     gradient = gradient_ref[...].astype(jnp.float32)
     wide_ref[...] = gradient
-    a1, a2, a3 = split_in_three(0.5 * momentum_ref[...] + gradient)
+    a1, a2, a3 = split_in_three(momentum_ref[...] + (gradient + near_ref[...]))
     left, right = jnp.concatenate([a1, a2], axis=1), jnp.concatenate([a1, a3], axis=1)
 
     def product(a, b):
@@ -279,7 +337,7 @@
 
     halves = []
     for half in range(2):
-        basis = jnp.where(core_ref[0] == half, own_ref[...], other_ref[...])
+        basis = jnp.where(place_ref[0] == half, own_ref[...], other_ref[...])
         b1, b2, b3 = split_in_three(basis)
         halves.append(
             product(left, jnp.concatenate([b1, b1], axis=1))
@@ -291,46 +349,62 @@
     term_ref[...] = jnp.concatenate(halves, axis=1)
 
 
-def sketch_term(core, momentum, gradient, own, other):
-    rows, columns = momentum.shape
-    step = rows // 4
+def sketch_term(place, momentum, gradient, near, own, other):
+    rows, columns = near.shape
+    steps = 2
+    step = rows // steps
+
+    def in_half(width):
+        return pl.BlockSpec((step, width), lambda i, place: (i + steps * place[1], 0))
 
     def by_rows(width):
-        return pl.BlockSpec((step, width), lambda i, core: (i, 0))
+        return pl.BlockSpec((step, width), lambda i, place: (i, 0))
 
     def whole(array):
-        return pl.BlockSpec(array.shape, lambda i, core: (0, 0))
+        return pl.BlockSpec(array.shape, lambda i, place: (0, 0))
 
     return pl.pallas_call(
         term_kernel,
         compiler_params=pltpu.CompilerParams(vmem_limit_bytes=KERNEL_VMEM),
         grid_spec=pltpu.PrefetchScalarGridSpec(
             num_scalar_prefetch=1,
-            grid=(rows // step,),
-            in_specs=[by_rows(columns), by_rows(columns), whole(own), whole(other)],
+            grid=(steps,),
+            in_specs=[
+                in_half(columns),
+                in_half(columns),
+                by_rows(columns),
+                whole(own),
+                whole(other),
+            ],
             out_specs=(by_rows(RANK), by_rows(columns)),
         ),
         out_shape=(
             jax.ShapeDtypeStruct((rows, RANK), jnp.float32),
             jax.ShapeDtypeStruct((rows, columns), jnp.float32),
         ),
-    )(core, in_hbm(momentum), in_hbm(gradient), in_hbm(own), other)
+    )(place, in_hbm(momentum), in_hbm(gradient), near, in_hbm(own), other)
 
 
 def step(weight, momentum, right_basis, gradients):
     share = len(right_basis)
     core = jnp.reshape(lax.axis_index("fsdp"), (1,)).astype(jnp.int32)
+    replica = jnp.reshape(lax.axis_index("dp"), (1,)).astype(jnp.int32)
     own = gradients[0, 0]
-    term, gradient = sketch_term(core, momentum, own, right_basis, swapped(right_basis, "fsdp"))
-    sketch = sum_at_owner(term, PLANE)
-    gradient, sketch = lax.optimization_barrier((gradient, sketch))
-    other = swapped(gradient, "dp")
-    sketch = sum_at_owner(sketch, "z")
-    sketch = gather(sketch, "z")
-    other, sketch = lax.optimization_barrier((other, sketch))
-    sketch = gather(sketch, PLANE)
-
-    gram, product, total = moments(sketch, momentum, own, other)
+    half = len(own) // 2
+    sent = lax.dynamic_slice_in_dim(own, (1 - lax.axis_index("dp")) * half, half, 0)
+    near = swapped(sent.astype(jnp.float32), "dp")
+    other_basis = swapped(right_basis, "fsdp")
+    term, wide = sketch_term(
+        jnp.concatenate([core, replica]), momentum, own, near, right_basis, other_basis
+    )
+    sketch = sum_at_owner(term, ("zl", "y", "xl"))
+    wide, sketch = lax.optimization_barrier((wide, sketch))
+    far = swapped(wide, "dp")
+    sketch = sent_to_all(sketch, "zh").sum(axis=0)
+    far, sketch = lax.optimization_barrier((far, sketch))
+    sketch = gather(sketch, NEAR)
+
+    gram, product, total = moments(replica, sketch, momentum, own, near, far)
     inverse, coefficients, squares = small_part(
         gram, swapped(gram, "fsdp"), product, swapped(product, "fsdp"), lax.axis_size(TENSOR)
     )
@@ -342,7 +416,7 @@
 
 
 def solution(mesh):
-    fine = Mesh(mesh.devices.reshape(2, 2, 8, 4, 2), ("dp", "fsdp", "z", "y", "xl"))
+    fine = Mesh(mesh.devices.reshape(2, 2, 4, 2, 4, 2), ("dp", "fsdp", *TENSOR))
     placed = P("fsdp", TENSOR)
     return jax.shard_map(
         step,

time: 156 us -> 132 us (0.85)
  blocking collectives: 87.9 us -> 65.8 us
  Pallas kernels: 38.9 us -> 25 us
  waiting for transfers between devices: 12 us -> 20.3 us
  starting transfers between devices: 16.1 us -> 17.9 us
    all_to_all x2 -> x1, blocking collectives: 48.3 us -> 21.3 us  [sum_at_owner(): return lax.all_to_all(pieces, axis, 0, 0, tiled=True).sum(axis=0)]
    pallas_call x1, Pallas kernels: 25 us -> 12.1 us  [small_part(): pl.pallas_call(coefficients_kernel, compiler_params=pltpu.CompilerParams(...]
    ppermute x4 -> x5, waiting for transfers between devices: 2.45 us -> 10.7 us  [swapped(): return lax.ppermute(value, axis, [(0, 1), (1, 0)])]
    all_to_all x2, blocking collectives: 39.6 us -> 44.5 us  [sent_to_all(): lax.all_to_all(jnp.broadcast_to(value[None], (length, *value.shape)), axi...]
    ppermute x4 -> x5, starting transfers between devices: 8.95 us -> 13 us  [swapped(): return lax.ppermute(value, axis, [(0, 1), (1, 0)])]
    all_to_all x1, starting transfers between devices: 7.18 us -> 4.93 us  [step(): squares = lax.all_to_all(squares, TENSOR, 0, 0, tiled=True)]
  transfers between devices with their start and end apart: 5 -> 6, of which waited for: 3 -> 4; matrix products, arithmetic and copies ran while one was open for 0% -> 0% of each run, Pallas kernels for 0% -> 0%
where the time goes in v1:
time: 132 us; the launch traced here: 131 us
  blocking collectives  65.8 us (50%)
  Pallas kernels  25 us (19%)
  waiting for transfers between devices  20.3 us (15%)
  starting transfers between devices  17.9 us (14%)
    all_to_all x2, blocking collectives, sent_to_all(): lax.all_to_all(jnp.broadcast_to(value[None], (length, *value.shape)), axi...  44.5 us
    all_to_all x1, blocking collectives, sum_at_owner(): return lax.all_to_all(pieces, axis, 0, 0, tiled=True).sum(axis=0)  21.3 us
    ppermute x5, starting transfers between devices, swapped(): return lax.ppermute(value, axis, [(0, 1), (1, 0)])  13 us
    pallas_call x1, Pallas kernels, small_part(): pl.pallas_call(coefficients_kernel, compiler_params=pltpu.CompilerParams(...  12.1 us
    ppermute x5, waiting for transfers between devices, swapped(): return lax.ppermute(value, axis, [(0, 1), (1, 0)])  10.7 us
    all_to_all x1, waiting for transfers between devices, step(): squares = lax.all_to_all(squares, TENSOR, 0, 0, tiled=True)  9.59 us
    pallas_call x1, Pallas kernels, updates(): pl.pallas_call(update_kernel, compiler_params=pltpu.CompilerParams(vmem_l...  5.19 us
    pallas_call x1, Pallas kernels, moments(): pl.pallas_call(moments_kernel, compiler_params=pltpu.CompilerParams(vmem_...  4.94 us
  transfers between devices with their start and end apart: 6, of which 4 were waited for; matrix products, arithmetic and copies ran while one was open for 0% of the time, Pallas kernels for 0%

profile of v1, /device:TPU:1, one launch (start us, length us, event | category | flops | bytes accessed | tf_op | source)
XLA Modules:
  0.0 131.1 jit_solution(270393595851365098)
XLA Ops:
  0.6 1.0 bitcast_convert_fusion
  1.6 3.6 %collective-permute-start = (f32[1024,128]{1,0:T(8,128)S(1)}, f32[1024,128]{1,0:T(8,128)S(1)}, u32[]{:S(2)}, u32[]{:S(2)}) collective-permute-start(f32[1024,128]{1,0:T(8,128)S(1)} %bitcast_convert_fusion), channel_id=1, source_target_pairs={{0,128},{128,0},{1,129},{129,1},{2,130},{130,2},{3,131},{131,3},{4... | collective-permute-start | bytes 1572872 | tf_op jit(solution)/shard_map/ppermute | solution.py:40
  5.3 1.0 collective-permute-start.1
  6.2 0.1 pad_add_fusion.place_ref
  6.3 1.0 collective-permute-done.1.other_ref
  7.3 8.5 %collective-permute-done.near_ref = f32[1024,128]{1,0:T(8,128)S(1)} collective-permute-done((f32[1024,128]{1,0:T(8,128)S(1)}, f32[1024,128]{1,0:T(8,128)S(1)}, u32[]{:S(2)}, u32[]{:S(2)}) %collective-permute-start) | collective-permute-done | bytes 524320 | tf_op jit(solution)/shard_map/ppermute | solution.py:40
  15.9 2.8 %shard_map.67 = (f32[1024,256]{1,0:T(8,128)S(1)}, f32[1024,128]{1,0:T(8,128)S(1)}) custom-call(s32[2]{0:T(128)S(1)} %pad_add_fusion.place_ref, f32[2048,128]{1,0:T(8,128)} %momentum_ref.3, bf16[2048,128]{1,0:T(8,128)(2,1)} %bitcast.11, f32[1024,128]{1,0:T(8,128)S(1)} %collective-permute-done.near_ref, f32[128,128]{1,0:T(8,128)} %own_ref.1, ...), custom_call_target="tpu_custom_call" | custom-call | tf_op jit(solution)/shard_map/pallas_call | solution.py:366
  18.7 21.3 %all_to_all.20 = f32[16,64,256]{2,1,0:T(8,128)S(1)} all-to-all(f32[16,64,256]{2,1,0:T(8,128)S(1)} %bitcast.10), channel_id=1, replica_groups=mesh['dp'=2,'fsdp'=2,'zh'=4,'zl'=2,'y'=4,'xl'=2] {'zl','y','xl'}, dimensions={0} | all-to-all | bytes 2097152 | tf_op jit(solution)/shard_map/all_to_all | solution.py:53
  40.0 0.1 reduce_sum.18
  40.0 2.5 %collective-permute-start.2 = (f32[1024,128]{1,0:T(8,128)S(1)}, f32[1024,128]{1,0:T(8,128)S(1)}, u32[]{:S(2)}, u32[]{:S(2)}) collective-permute-start(f32[1024,128]{1,0:T(8,128)S(1)} %get-tuple-element.17), channel_id=1, source_target_pairs={{0,128},{128,0},{1,129},{129,1},{2,130},{130,2},{3,131},{131,3},{4... | collective-permute-start | bytes 1572872 | tf_op jit(solution)/shard_map/ppermute | solution.py:40
  42.6 15.4 %all_to_all.21 = f32[4,64,256]{2,1,0:T(8,128)S(1)} all-to-all(f32[4,64,256]{2,1,0:T(8,128)S(1)} %broadcast_in_dim.4), channel_id=1, replica_groups=mesh['dp'=2,'fsdp'=2,'zh'=4,'zl'=2,'y'=4,'xl'=2] {'zh'}, dimensions={0} | all-to-all | bytes 524288 | tf_op jit(solution)/shard_map/all_to_all | solution.py:45
  58.0 0.0 collective-permute-done.2.far_ref
  58.0 0.2 broadcast_in_dim.5
  58.3 29.1 %all_to_all.22 = f32[32,64,256]{2,1,0:T(8,128)S(1)} all-to-all(f32[32,64,256]{2,1,0:T(8,128)S(1)} %broadcast_in_dim.5), channel_id=1, replica_groups=mesh['dp'=2,'fsdp'=2,'zh'=4,'zl'=2,'y'=4,'xl'=2] {'dp','zl','y','xl'}, dimensions={0} | all-to-all | bytes 4194304 | tf_op jit(solution)/shard_map/all_to_all | solution.py:45
  87.3 4.9 %shard_map.68 = (f32[256,256]{1,0:T(8,128)S(1)}, f32[256,128]{1,0:T(8,128)S(1)}, f32[2048,128]{1,0:T(8,128)}) custom-call(s32[1]{0:T(128)} %bitcast.1.replica_ref, f32[2048,256]{1,0:T(8,128)S(1)} %bitcast.8, f32[2048,128]{1,0:T(8,128)} %momentum_ref.3, bf16[2048,128]{1,0:T(8,128)(2,1)} %bitcast.12, f32[1024,128]{1,0:T(8,128)S(1)} %collective-permute-done.near_ref, ...), custom_call_target="tpu_custom_call" | custom-call | tf_op jit(solution)/shard_map/pallas_call | solution.py:178
  92.3 5.7 %collective-permute-start.3 = (f32[256,256]{1,0:T(8,128)S(1)}, f32[256,256]{1,0:T(8,128)S(1)}, u32[]{:S(2)}, u32[]{:S(2)}) collective-permute-start(f32[256,256]{1,0:T(8,128)S(1)} %get-tuple-element.21.gram_ref), channel_id=1, source_target_pairs={{0,64},{64,0},{1,65},{65,1},{2,66},{66,2},{3,67},{67,3},{4,68},{68... | collective-permute-start | bytes 786440 | tf_op jit(solution)/shard_map/ppermute | solution.py:40
  97.9 0.2 collective-permute-start.4
  98.1 1.2 collective-permute-done.4.other_product_ref
  99.3 0.0 collective-permute-done.3.other_gram_ref
  99.3 12.1 %shard_map.69 = (f32[256,256]{1,0:T(8,128)}, f32[256,128]{1,0:T(8,128)}, f32[64,1,256]{2,1,0:T(1,128)}) custom-call(f32[256,256]{1,0:T(8,128)S(1)} %get-tuple-element.21.gram_ref, f32[256,256]{1,0:T(8,128)S(1)} %collective-permute-done.3.other_gram_ref, f32[256,128]{1,0:T(8,128)S(1)} %get-tuple-element.22.product_ref, ...), custom_call_target="tpu_custom_call" | custom-call | tf_op jit(solution)/shard_map/pallas_call | solution.py:236
  111.4 4.9 %all-to-all-start.3 = ((f32[64,1,256]{2,1,0:T(1,128)}), f32[64,1,256]{2,1,0:T(1,128)S(1)}, u32[]{:S(2)}, u32[]{:S(2)}) async-start(f32[64,1,256]{2,1,0:T(1,128)} %get-tuple-element.23), calls=%async_computation.3 | async-start | bytes 131072 | tf_op jit(solution)/shard_map/all_to_all | solution.py:411
  116.3 9.6 %all-to-all-done.3.squares_ref = f32[64,1,256]{2,1,0:T(1,128)S(1)} async-done(((f32[64,1,256]{2,1,0:T(1,128)}), f32[64,1,256]{2,1,0:T(1,128)S(1)}, u32[]{:S(2)}, u32[]{:S(2)}) %all-to-all-start.3) | async-done | bytes 65568 | tf_op jit(solution)/shard_map/all_to_all | solution.py:411
  125.9 5.2 %shard_map.70 = (f32[2048,128]{1,0:T(8,128)}, f32[2048,128]{1,0:T(8,128)}, f32[128,128]{1,0:T(8,128)}) custom-call(s32[1]{0:T(128)S(6)} %mul.6.first_ref, f32[64,1,256]{2,1,0:T(1,128)S(1)} %all-to-all-done.3.squares_ref, f32[2048,256]{1,0:T(8,128)S(1)} %bitcast.9, f32[256,256]{1,0:T(8,128)} %get-tuple-element.24.inverse_ref, ...), custom_call_target="tpu_custom_call" | custom-call | tf_op jit(solution)/shard_map/pallas_call | solution.py:287
  (2 shorter events, 0.0 us)
Async XLA Ops:
  1.6 14.3 %collective-permute-start = (f32[1024,128]{1,0:T(8,128)S(1)}, f32[1024,128]{1,0:T(8,128)S(1)}, u32[]{:S(2)}, u32[]{:S(2)}) collective-permute-start(f32[1024,128]{1,0:T(8,128)S(1)} %bitcast_convert_fusion), channel_id=1, source_target_pairs={{0,128},{128,0},{1,129},{129,1},{2,130},{130,2},{3,131},{131,3},{4... | collective-permute-start | bytes 1572872 | tf_op jit(solution)/shard_map/ppermute | solution.py:40
  5.3 2.1 %collective-permute-start.1 = (f32[128,128]{1,0:T(8,128)}, f32[128,128]{1,0:T(8,128)S(1)}, u32[]{:S(2)}, u32[]{:S(2)}) collective-permute-start(f32[128,128]{1,0:T(8,128)} %own_ref.1), channel_id=1, source_target_pairs={{0,64},{64,0},{1,65},{65,1},{2,66},{66,2},{3,67},{67,3},{4,68},{68... | collective-permute-start | bytes 196616 | tf_op jit(solution)/shard_map/ppermute | solution.py:40
  40.0 18.0 %collective-permute-start.2 = (f32[1024,128]{1,0:T(8,128)S(1)}, f32[1024,128]{1,0:T(8,128)S(1)}, u32[]{:S(2)}, u32[]{:S(2)}) collective-permute-start(f32[1024,128]{1,0:T(8,128)S(1)} %get-tuple-element.17), channel_id=1, source_target_pairs={{0,128},{128,0},{1,129},{129,1},{2,130},{130,2},{3,131},{131,3},{4... | collective-permute-start | bytes 1572872 | tf_op jit(solution)/shard_map/ppermute | solution.py:40
  92.3 7.0 %collective-permute-start.3 = (f32[256,256]{1,0:T(8,128)S(1)}, f32[256,256]{1,0:T(8,128)S(1)}, u32[]{:S(2)}, u32[]{:S(2)}) collective-permute-start(f32[256,256]{1,0:T(8,128)S(1)} %get-tuple-element.21.gram_ref), channel_id=1, source_target_pairs={{0,64},{64,0},{1,65},{65,1},{2,66},{66,2},{3,67},{67,3},{4,68},{68... | collective-permute-start | bytes 786440 | tf_op jit(solution)/shard_map/ppermute | solution.py:40
  97.9 1.3 %collective-permute-start.4 = (f32[256,128]{1,0:T(8,128)S(1)}, f32[256,128]{1,0:T(8,128)S(1)}, u32[]{:S(2)}, u32[]{:S(2)}) collective-permute-start(f32[256,128]{1,0:T(8,128)S(1)} %get-tuple-element.22.product_ref), channel_id=1, source_target_pairs={{0,64},{64,0},{1,65},{65,1},{2,66},{66,2},{3,67},{67,3},{4,68},{68... | collective-permute-start | bytes 393224 | tf_op jit(solution)/shard_map/ppermute | solution.py:40
  111.4 14.5 %all-to-all-start.3 = ((f32[64,1,256]{2,1,0:T(1,128)}), f32[64,1,256]{2,1,0:T(1,128)S(1)}, u32[]{:S(2)}, u32[]{:S(2)}) async-start(f32[64,1,256]{2,1,0:T(1,128)} %get-tuple-element.23), calls=%async_computation.3 | async-start | bytes 131072 | tf_op jit(solution)/shard_map/all_to_all | solution.py:411

commit v2 on v1

--- a/solution.py
+++ b/solution.py
@@ -142,65 +142,50 @@
 
 
 def moments_kernel(
-    replica_ref, sketch_ref, momentum_ref, own_ref, near_ref, far_ref,
-    gram_ref, product_ref, total_ref,
+    replica_ref, sketch_ref, momentum_ref, own_ref, near_ref, far_ref, gram_ref, product_ref
 ):
-    step = pl.program_id(0)
-
-    @pl.when(step == 0)
-    def _():
-        gram_ref[...] = jnp.zeros_like(gram_ref)
-        product_ref[...] = jnp.zeros_like(product_ref)
-
-    sketch = sketch_ref[...]
-    in_own_half = step // (pl.num_programs(0) // 2) == replica_ref[0]
-    other = jnp.where(in_own_half, near_ref[...], far_ref[...])
-    total = momentum_ref[...] + (own_ref[...].astype(jnp.float32) + other)
-    total_ref[...] = total
-    gram_ref[...] += contract(sketch, sketch, 0, 0)
-    product_ref[...] += three_pass(sketch, total, 0, 0)
+    def product(a, b):
+        return lax.dot_general(
+            a, b, (((0,), (0,)), ((), ())), preferred_element_type=jnp.float32
+        )
+
+    half = near_ref.shape[0]
+    steps = 2
+    step = half // steps
+    gram, one_side, moved = 0.0, 0.0, 0.0
+    for part in range(2):
+        for i in range(steps):
+            rows = pl.ds(part * half + i * step, step)
+            within = pl.ds(i * step, step)
+            other = jnp.where(replica_ref[0] == part, near_ref[within, :], far_ref[within, :])
+            total = momentum_ref[rows, :] + (own_ref[rows, :].astype(jnp.float32) + other)
+            a1, a2, a3 = split_in_three(sketch_ref[rows, :])
+            b1, b2 = split(total)
+            one_side += product(a1, a2) + product(a1, a3)
+            gram += product(a1, a1) + product(a2, a2)
+            moved += product(a1, b1) + (product(a1, b2) + product(a2, b1))
+    gram_ref[...] = gram + (one_side + one_side.T)
+    product_ref[...] = moved
 
 
 def moments(replica, sketch, momentum, own, near, far):
-    rows, columns = momentum.shape
-    steps = 4
-    step = rows // steps
-
-    def by_rows(width):
-        return pl.BlockSpec((step, width), lambda i, replica: (i, 0))
-
-    def by_half(width):
-        return pl.BlockSpec((step, width), lambda i, replica: (i % (steps // 2), 0))
-
-    def whole(*shape):
-        return pl.BlockSpec(shape, lambda i, replica: (0, 0))
-
+    columns = momentum.shape[1]
     return pl.pallas_call(
         moments_kernel,
         compiler_params=pltpu.CompilerParams(vmem_limit_bytes=KERNEL_VMEM),
-        grid_spec=pltpu.PrefetchScalarGridSpec(
-            num_scalar_prefetch=1,
-            grid=(steps,),
-            in_specs=[
-                by_rows(RANK),
-                by_rows(columns),
-                by_rows(columns),
-                by_half(columns),
-                by_half(columns),
-            ],
-            out_specs=(whole(RANK, RANK), whole(RANK, columns), by_rows(columns)),
-        ),
         out_shape=(
             jax.ShapeDtypeStruct((RANK, RANK), jnp.float32),
             jax.ShapeDtypeStruct((RANK, columns), jnp.float32),
-            pltpu.HBM((rows, columns), jnp.float32),
-        ),
-    )(replica, sketch, in_hbm(momentum), in_hbm(own), near, far)
+        ),
+        in_specs=[pl.BlockSpec(memory_space=pltpu.SMEM)]
+        + [pl.BlockSpec(memory_space=pltpu.VMEM)] * 5,
+        out_specs=(pl.BlockSpec(memory_space=pltpu.VMEM),) * 2,
+    )(replica, sketch, momentum, own, near, far)
 
 
 def coefficients_kernel(
     gram_ref, other_gram_ref, product_ref, other_product_ref,
-    inverse_ref, coefficients_ref, squares_ref, held,
+    inverse_ref, coefficients_ref, change_ref, squares_ref, held,
 ):
     held[...] = gram_ref[...] + other_gram_ref[...]
     for first in range(0, RANK, BLOCK):
@@ -223,7 +208,9 @@
     inverse = jnp.where(lane <= row, held[...], 0.0)
     coefficients = contract(inverse, product_ref[...] + other_product_ref[...], 1, 0)
     coefficients_ref[...] = coefficients
-    inverse_ref[...] = inverse.T
+    inverse = inverse.T
+    inverse_ref[...] = inverse
+    change_ref[...] = drop_share * contract(inverse, coefficients, 1, 0)
     ones = jnp.ones((8, coefficients.shape[1]), jnp.float32)
     squares = contract(ones, coefficients * coefficients, 1, 1)
     squares_ref[...] = jnp.broadcast_to(squares[None, :1], squares_ref.shape)
@@ -239,80 +226,118 @@
         out_shape=(
             pltpu.HBM(gram.shape, jnp.float32),
             pltpu.HBM(product.shape, jnp.float32),
+            pltpu.HBM(product.shape, jnp.float32),
             jax.ShapeDtypeStruct((copies, 1, RANK), jnp.float32),
         ),
         in_specs=[pl.BlockSpec(memory_space=pltpu.VMEM)] * 4,
         grid=(1,),
-        out_specs=(whole(gram.shape), whole(product.shape), whole((copies, 1, RANK))),
+        out_specs=(
+            whole(gram.shape),
+            whole(product.shape),
+            whole(product.shape),
+            whole((copies, 1, RANK)),
+        ),
         scratch_shapes=[pltpu.VMEM((RANK, RANK), jnp.float32)],
     )(gram, other_gram, product, other_product)
 
 
-def update_kernel(
-    first_ref, squares_ref, sketch_ref, inverse_ref, coefficients_ref, weight_ref, total_ref,
-    weight_out_ref, momentum_out_ref, basis_ref, change_ref,
+def momentum_kernel(
+    replica_ref, sketch_ref, change_ref, momentum_ref, own_ref, near_ref, far_ref, out_ref
 ):
-    columns = weight_ref.shape[1]
-
-    @pl.when(pl.program_id(0) == 0)
-    def _():
-        step_scale = step_size * math.sqrt(ROWS * D / RANK)
-        scale = lax.rsqrt(jnp.sum(squares_ref[:, 0, :], axis=0, keepdims=True) + guard_term)
-        inverse = inverse_ref[...]
-        coefficients = coefficients_ref[...]
-        change_ref[:, :columns] = step_scale * contract(inverse * scale, coefficients, 1, 0)
-        change_ref[:, columns:] = drop_share * contract(inverse, coefficients, 1, 0)
-        share = basis_ref.shape[0]
-        row = lax.broadcasted_iota(jnp.int32, (share, RANK), 0) + first_ref[0]
-        lane = lax.broadcasted_iota(jnp.int32, (share, RANK), 1)
-        column = jnp.sum(jnp.where(row == lane, scale, 0.0), axis=1, keepdims=True)
-        first = pl.multiple_of(first_ref[0], share)
-        basis_ref[...] = coefficients_ref[pl.ds(first, share), :] * column
-
-    change = three_pass(sketch_ref[...], change_ref[...], 1, 0)
-    weight_out_ref[...] = weight_ref[...] - change[:, :columns]
-    momentum_out_ref[...] = total_ref[...] - change[:, columns:]
-
-
-def updates(first, squares, sketch, inverse, coefficients, weight, total, share):
-    rows, columns = weight.shape
-    step = rows // 4
-
-    def whole(array):
-        return pl.BlockSpec(array.shape, lambda i, first: (0,) * array.ndim)
+    in_own_half = pl.program_id(0) // (pl.num_programs(0) // 2) == replica_ref[0]
+    other = jnp.where(in_own_half, near_ref[...], far_ref[...])
+    total = momentum_ref[...] + (own_ref[...].astype(jnp.float32) + other)
+    out_ref[...] = total - three_pass(sketch_ref[...], change_ref[...], 1, 0)
+
+
+def new_momentum(replica, sketch, change, momentum, own, near, far):
+    rows, columns = momentum.shape
+    steps = 4
+    step = rows // steps
 
     def by_rows(width):
-        return pl.BlockSpec((step, width), lambda i, first: (i, 0))
-
-    return pl.pallas_call(
-        update_kernel,
+        return pl.BlockSpec((step, width), lambda i, replica: (i, 0))
+
+    def by_half(width):
+        return pl.BlockSpec((step, width), lambda i, replica: (i % (steps // 2), 0))
+
+    return pl.pallas_call(
+        momentum_kernel,
         compiler_params=pltpu.CompilerParams(vmem_limit_bytes=KERNEL_VMEM),
         grid_spec=pltpu.PrefetchScalarGridSpec(
             num_scalar_prefetch=1,
-            grid=(rows // step,),
+            grid=(steps,),
             in_specs=[
-                whole(squares),
                 by_rows(RANK),
-                whole(inverse),
-                whole(coefficients),
+                pl.BlockSpec((RANK, columns), lambda i, replica: (0, 0)),
                 by_rows(columns),
                 by_rows(columns),
+                by_half(columns),
+                by_half(columns),
             ],
-            out_specs=(
-                by_rows(columns),
-                by_rows(columns),
-                pl.BlockSpec((share, columns), lambda i, first: (0, 0)),
-            ),
-            scratch_shapes=[pltpu.VMEM((RANK, 2 * columns), jnp.float32)],
-        ),
+            out_specs=by_rows(columns),
+        ),
+        out_shape=jax.ShapeDtypeStruct(momentum.shape, jnp.float32),
+        cost_estimate=pl.CostEstimate(
+            flops=6 * rows * RANK * columns,
+            bytes_accessed=4 * rows * (RANK + 2 * columns),
+            transcendentals=0,
+        ),
+    )(replica, sketch, in_hbm(change), in_hbm(momentum), in_hbm(own), in_hbm(near), in_hbm(far))
+
+
+def weight_kernel(
+    first_ref, squares_ref, sketch_ref, inverse_ref, coefficients_ref, weight_ref,
+    out_ref, basis_ref, near_coefficients, held, arrived, done,
+):
+    arrival = pltpu.make_async_copy(coefficients_ref, near_coefficients, arrived)
+    arrival.start()
+    step_scale = step_size * math.sqrt(ROWS * D / RANK)
+    scale = lax.rsqrt(jnp.sum(squares_ref[:, 0, :], axis=0, keepdims=True) + guard_term)
+    scaled = inverse_ref[...] * scale
+    arrival.wait()
+    change = step_scale * contract(scaled, near_coefficients[...], 1, 0)
+    steps, step, _ = held.shape
+    copies = []
+    for i in range(steps):
+        rows = pl.ds(i * step, step)
+        held[i] = weight_ref[rows, :] - three_pass(sketch_ref[rows, :], change, 1, 0)
+        copies.append(pltpu.make_async_copy(held.at[i], out_ref.at[rows, :], done.at[i]))
+        copies[-1].start()
+    share = basis_ref.shape[0]
+    row = lax.broadcasted_iota(jnp.int32, (share, RANK), 0) + first_ref[0]
+    lane = lax.broadcasted_iota(jnp.int32, (share, RANK), 1)
+    column = jnp.sum(jnp.where(row == lane, scale, 0.0), axis=1, keepdims=True)
+    first = pl.multiple_of(first_ref[0], share)
+    basis_ref[...] = near_coefficients[pl.ds(first, share), :] * column
+    for copy in copies:
+        copy.wait()
+
+
+def new_weight(first, squares, sketch, inverse, coefficients, weight, share):
+    rows, columns = weight.shape
+    steps = 8
+    return pl.pallas_call(
+        weight_kernel,
+        compiler_params=pltpu.CompilerParams(vmem_limit_bytes=KERNEL_VMEM),
         out_shape=(
             jax.ShapeDtypeStruct(weight.shape, jnp.float32),
-            jax.ShapeDtypeStruct(weight.shape, jnp.float32),
             jax.ShapeDtypeStruct((share, columns), jnp.float32),
         ),
-    )(
-        first, squares, sketch, in_hbm(inverse), in_hbm(coefficients), in_hbm(weight), in_hbm(total)
-    )
+        in_specs=[pl.BlockSpec(memory_space=pltpu.SMEM)]
+        + [pl.BlockSpec(memory_space=pltpu.VMEM)] * 3
+        + [pl.BlockSpec(memory_space=pl.ANY), pl.BlockSpec(memory_space=pltpu.VMEM)],
+        out_specs=(
+            pl.BlockSpec(memory_space=pl.ANY),
+            pl.BlockSpec(memory_space=pltpu.VMEM),
+        ),
+        scratch_shapes=[
+            pltpu.VMEM(coefficients.shape, jnp.float32),
+            pltpu.VMEM((steps, rows // steps, columns), jnp.float32),
+            pltpu.SemaphoreType.DMA,
+            pltpu.SemaphoreType.DMA((steps,)),
+        ],
+    )(first, squares, sketch, inverse, in_hbm(coefficients), weight)
 
 
 def split_in_three(value):
@@ -322,35 +347,45 @@
     return high, middle_part, (middle - middle_part.astype(jnp.float32)).astype(jnp.bfloat16)
 
 
-def term_kernel(
-    place_ref, momentum_ref, gradient_ref, near_ref, own_ref, other_ref, term_ref, wide_ref
-):
+def spread_basis(core, own, other, half):
+    return split_in_three(jnp.where(core == half, own, other))
+
+
+def pair(a, b):
+    return jnp.concatenate([a, b], axis=1)
+
+
+def row_product(a, b):
+    return lax.dot_general(a, b, (((1,), (1,)), ((), ())), preferred_element_type=jnp.float32)
+
+
+def first_term_kernel(place_ref, momentum_ref, gradient_ref, own_ref, other_ref, term_ref, wide_ref):
     gradient = gradient_ref[...].astype(jnp.float32)
     wide_ref[...] = gradient
-    a1, a2, a3 = split_in_three(momentum_ref[...] + (gradient + near_ref[...]))
-    left, right = jnp.concatenate([a1, a2], axis=1), jnp.concatenate([a1, a3], axis=1)
-
-    def product(a, b):
-        return lax.dot_general(
-            a, b, (((1,), (1,)), ((), ())), preferred_element_type=jnp.float32
+    a1, a2, a3 = split_in_three(momentum_ref[...] + gradient)
+    left, right = pair(a1, a2), pair(a1, a3)
+    for half in range(2):
+        b1, b2, b3 = spread_basis(place_ref[0], own_ref[...], other_ref[...], half)
+        share = own_ref.shape[0]
+        term_ref[:, half * share : half * share + share] = row_product(left, pair(b1, b1)) + (
+            row_product(left, pair(b2, b2)) + row_product(right, pair(b3, b1))
         )
 
-    halves = []
+
+def second_term_kernel(place_ref, near_ref, first_ref, own_ref, other_ref, term_ref):
+    near = near_ref[...].astype(jnp.bfloat16)
+    twice = pair(near, near)
     for half in range(2):
-        basis = jnp.where(place_ref[0] == half, own_ref[...], other_ref[...])
-        b1, b2, b3 = split_in_three(basis)
-        halves.append(
-            product(left, jnp.concatenate([b1, b1], axis=1))
-            + (
-                product(left, jnp.concatenate([b2, b2], axis=1))
-                + product(right, jnp.concatenate([b3, b1], axis=1))
-            )
+        b1, b2, b3 = spread_basis(place_ref[0], own_ref[...], other_ref[...], half)
+        share = own_ref.shape[0]
+        columns = slice(half * share, half * share + share)
+        term_ref[:, columns] = first_ref[:, columns] + (
+            row_product(twice, pair(b1, b2)) + row_product(near, b3)
         )
-    term_ref[...] = jnp.concatenate(halves, axis=1)
-
-
-def sketch_term(place, momentum, gradient, near, own, other):
-    rows, columns = near.shape
+
+
+def first_term(place, momentum, gradient, own, other):
+    rows, columns = len(momentum) // 2, momentum.shape[1]
     steps = 2
     step = rows // steps
 
@@ -364,25 +399,35 @@
         return pl.BlockSpec(array.shape, lambda i, place: (0, 0))
 
     return pl.pallas_call(
-        term_kernel,
+        first_term_kernel,
         compiler_params=pltpu.CompilerParams(vmem_limit_bytes=KERNEL_VMEM),
         grid_spec=pltpu.PrefetchScalarGridSpec(
             num_scalar_prefetch=1,
             grid=(steps,),
-            in_specs=[
-                in_half(columns),
-                in_half(columns),
-                by_rows(columns),
-                whole(own),
-                whole(other),
-            ],
+            in_specs=[in_half(columns), in_half(columns), whole(own), whole(other)],
             out_specs=(by_rows(RANK), by_rows(columns)),
         ),
         out_shape=(
             jax.ShapeDtypeStruct((rows, RANK), jnp.float32),
             jax.ShapeDtypeStruct((rows, columns), jnp.float32),
         ),
-    )(place, in_hbm(momentum), in_hbm(gradient), near, in_hbm(own), other)
+        cost_estimate=pl.CostEstimate(
+            flops=12 * rows * RANK * columns,
+            bytes_accessed=4 * rows * (RANK + 3 * columns),
+            transcendentals=0,
+        ),
+    )(place, in_hbm(momentum), in_hbm(gradient), in_hbm(own), other)
+
+
+def second_term(place, near, first, own, other):
+    return pl.pallas_call(
+        second_term_kernel,
+        compiler_params=pltpu.CompilerParams(vmem_limit_bytes=KERNEL_VMEM),
+        out_shape=jax.ShapeDtypeStruct(first.shape, jnp.float32),
+        in_specs=[pl.BlockSpec(memory_space=pltpu.SMEM)]
+        + [pl.BlockSpec(memory_space=pltpu.VMEM)] * 4,
+        out_specs=pl.BlockSpec(memory_space=pltpu.VMEM),
+    )(place, near, first, own, other)
 
 
 def step(weight, momentum, right_basis, gradients):
@@ -394,23 +439,25 @@
     sent = lax.dynamic_slice_in_dim(own, (1 - lax.axis_index("dp")) * half, half, 0)
     near = swapped(sent.astype(jnp.float32), "dp")
     other_basis = swapped(right_basis, "fsdp")
-    term, wide = sketch_term(
-        jnp.concatenate([core, replica]), momentum, own, near, right_basis, other_basis
-    )
+    place = jnp.concatenate([core, replica])
+    term, wide = first_term(place, momentum, own, right_basis, other_basis)
+    term = second_term(place, near, term, right_basis, other_basis)
     sketch = sum_at_owner(term, ("zl", "y", "xl"))
     wide, sketch = lax.optimization_barrier((wide, sketch))
     far = swapped(wide, "dp")
-    sketch = sent_to_all(sketch, "zh").sum(axis=0)
+    sketch = sketch + lax.ppermute(sketch, "zh", [(0, 1), (1, 0), (2, 3), (3, 2)])
+    sketch = sketch + lax.ppermute(sketch, "zh", [(0, 3), (3, 0), (1, 2), (2, 1)])
     far, sketch = lax.optimization_barrier((far, sketch))
     sketch = gather(sketch, NEAR)
 
-    gram, product, total = moments(replica, sketch, momentum, own, near, far)
-    inverse, coefficients, squares = small_part(
+    gram, product = moments(replica, sketch, momentum, own, near, far)
+    inverse, coefficients, change, squares = small_part(
         gram, swapped(gram, "fsdp"), product, swapped(product, "fsdp"), lax.axis_size(TENSOR)
     )
     squares = lax.all_to_all(squares, TENSOR, 0, 0, tiled=True)
-    weight, momentum, right_basis = updates(
-        core * share, squares, sketch, inverse, coefficients, weight, total, share
+    momentum = new_momentum(replica, sketch, change, momentum, own, near, far)
+    weight, right_basis = new_weight(
+        core * share, squares, sketch, inverse, coefficients, weight, share
     )
     return weight, momentum, right_basis
 

time: 132 us -> 127 us (0.962)
  blocking collectives: 65.8 us -> 52.2 us
  starting transfers between devices: 17.9 us -> 27.2 us
  waiting for transfers between devices: 20.3 us -> 17.3 us
  Pallas kernels: 25 us -> 27.2 us
    all_to_all x2 -> x1, blocking collectives: 44.5 us -> 30.9 us  [sent_to_all(): lax.all_to_all(jnp.broadcast_to(value[None], (length, *value.shape)), axi...]
    ppermute x0 -> x2, starting transfers between devices: none -> 6.57 us  [the longest x1 3.58 us: step(): lax.ppermute(sketch, 'zh', [(0, 3), (3, 0), (1, 2), (2, 1)])]
    all_to_all x1, waiting for transfers between devices: 9.59 us -> 4.75 us  [step(): squares = lax.all_to_all(squares, TENSOR, 0, 0, tiled=True)]
    pallas_call x2 -> x4, Pallas kernels: 7.95 us -> 12.7 us  [the longest x1 4.83 us: new_momentum(): pl.pallas_call(momentum_kernel, compiler_params=pltpu.CompilerParams(vmem...]
    ppermute x0 -> x2, waiting for transfers between devices: none -> 4.67 us  [the longest x1 2.65 us: step(): lax.ppermute(sketch, 'zh', [(0, 1), (1, 0), (2, 3), (3, 2)])]
    all_to_all x1, starting transfers between devices: 4.93 us -> 8.27 us  [step(): squares = lax.all_to_all(squares, TENSOR, 0, 0, tiled=True)]
    ppermute x5, waiting for transfers between devices: 10.7 us -> 7.88 us  [swapped(): return lax.ppermute(value, axis, [(0, 1), (1, 0)])]
    pallas_call x1, Pallas kernels: 4.94 us -> 2.13 us  [moments(): pl.pallas_call(moments_kernel, compiler_params=pltpu.CompilerParams(vmem_...]
  transfers between devices with their start and end apart: 6 -> 8, of which waited for: 4 -> 6; matrix products, arithmetic and copies ran while one was open for 0% -> 0% of each run, Pallas kernels for 0% -> 6%
where the time goes in v2:
time: 127 us; the launch traced here: 126 us
  blocking collectives  52.2 us (41%)
  starting transfers between devices  27.2 us (21%)
  Pallas kernels  27.2 us (21%)
  waiting for transfers between devices  17.3 us (14%)
    all_to_all x1, blocking collectives, sent_to_all(): lax.all_to_all(jnp.broadcast_to(value[None], (length, *value.shape)), axi...  30.9 us
    all_to_all x1, blocking collectives, sum_at_owner(): return lax.all_to_all(pieces, axis, 0, 0, tiled=True).sum(axis=0)  21.3 us
    pallas_call x1, Pallas kernels, small_part(): pl.pallas_call(coefficients_kernel, compiler_params=pltpu.CompilerParams(...  12.4 us
    ppermute x5, starting transfers between devices, swapped(): return lax.ppermute(value, axis, [(0, 1), (1, 0)])  12.4 us
    all_to_all x1, starting transfers between devices, step(): squares = lax.all_to_all(squares, TENSOR, 0, 0, tiled=True)  8.27 us
    ppermute x5, waiting for transfers between devices, swapped(): return lax.ppermute(value, axis, [(0, 1), (1, 0)])  7.88 us
    pallas_call x1, Pallas kernels, new_momentum(): pl.pallas_call(momentum_kernel, compiler_params=pltpu.CompilerParams(vmem...  4.83 us
    all_to_all x1, waiting for transfers between devices, step(): squares = lax.all_to_all(squares, TENSOR, 0, 0, tiled=True)  4.75 us
  transfers between devices with their start and end apart: 8, of which 6 were waited for; matrix products, arithmetic and copies ran while one was open for 0% of the time, Pallas kernels for 6%

profile of v2, /device:TPU:1, one launch (start us, length us, event | category | flops | bytes accessed | tf_op | source)
XLA Modules:
  0.0 126.3 jit_solution(13674500004155653093)
XLA Ops:
  0.6 0.0 copy-start.6
  0.6 1.0 bitcast_convert_fusion
  1.7 3.6 %collective-permute-start.1 = (f32[1024,128]{1,0:T(8,128)S(1)}, f32[1024,128]{1,0:T(8,128)S(1)}, u32[]{:S(2)}, u32[]{:S(2)}) collective-permute-start(f32[1024,128]{1,0:T(8,128)S(1)} %bitcast_convert_fusion), channel_id=1, source_target_pairs={{0,128},{128,0},{1,129},{129,1},{2,130},{130,2},{3,131},{131,3},{4... | collective-permute-start | bytes 1572872 | tf_op jit(solution)/shard_map/ppermute | solution.py:40
  5.3 1.0 collective-permute-start
  6.3 0.1 pad_add_fusion.place_ref
  6.4 1.0 collective-permute-done.other_ref
  7.4 2.8 %shard_map.67 = (f32[1024,256]{1,0:T(8,128)S(1)}, f32[1024,128]{1,0:T(8,128)S(1)}) custom-call(s32[2]{0:T(128)S(1)} %pad_add_fusion.place_ref, f32[2048,128]{1,0:T(8,128)} %momentum_ref.5, bf16[2048,128]{1,0:T(8,128)(2,1)} %bitcast.11, f32[128,128]{1,0:T(8,128)} %own_ref.3, f32[128,128]{1,0:T(8,128)S(1)} %collective-permute-done.other_ref), custom_call_target="tpu_custom_call" | custom-call | flops 402653184 | bytes 2621440 | tf_op jit(solution)/shard_map/pallas_call | solution.py:401
  10.2 5.8 %collective-permute-done.1.near_ref = f32[1024,128]{1,0:T(8,128)S(1)} collective-permute-done((f32[1024,128]{1,0:T(8,128)S(1)}, f32[1024,128]{1,0:T(8,128)S(1)}, u32[]{:S(2)}, u32[]{:S(2)}) %collective-permute-start.1) | collective-permute-done | bytes 524320 | tf_op jit(solution)/shard_map/ppermute | solution.py:40
  15.9 0.0 copy-start.2
  15.9 0.0 copy-done.6
  15.9 1.1 shard_map.68
  17.1 21.3 %all_to_all.15 = f32[16,64,256]{2,1,0:T(8,128)S(1)} all-to-all(f32[16,64,256]{2,1,0:T(8,128)S(1)} %bitcast.14), channel_id=1, replica_groups=mesh['dp'=2,'fsdp'=2,'zh'=4,'zl'=2,'y'=4,'xl'=2] {'zl','y','xl'}, dimensions={0} | all-to-all | bytes 2097152 | tf_op jit(solution)/shard_map/all_to_all | solution.py:53
  38.4 0.0 copy-done.2
  38.4 0.1 reduce_sum.9
  38.5 2.5 %collective-permute-start.2 = (f32[1024,128]{1,0:T(8,128)S(1)}, f32[1024,128]{1,0:T(8,128)S(1)}, u32[]{:S(2)}, u32[]{:S(2)}) collective-permute-start(f32[1024,128]{1,0:T(8,128)S(1)} %get-tuple-element.19), channel_id=1, source_target_pairs={{0,128},{128,0},{1,129},{129,1},{2,130},{130,2},{3,131},{131,3},{4... | collective-permute-start | bytes 1572872 | tf_op jit(solution)/shard_map/ppermute | solution.py:40
  41.0 3.0 %collective-permute-start.3 = (f32[64,256]{1,0:T(8,128)S(1)}, f32[64,256]{1,0:T(8,128)S(1)}, u32[]{:S(2)}, u32[]{:S(2)}) collective-permute-start(f32[64,256]{1,0:T(8,128)S(1)} %reduce_sum.9), channel_id=1, source_target_pairs={{0,16},{16,0},{32,48},{48,32},{1,17},{17,1},{33,49},{49,33},{2,18}... | collective-permute-start | bytes 196616 | tf_op jit(solution)/shard_map/ppermute | solution.py:448
  44.0 2.6 %collective-permute-done.3 = f32[64,256]{1,0:T(8,128)S(1)} collective-permute-done((f32[64,256]{1,0:T(8,128)S(1)}, f32[64,256]{1,0:T(8,128)S(1)}, u32[]{:S(2)}, u32[]{:S(2)}) %collective-permute-start.3) | collective-permute-done | bytes 65568 | tf_op jit(solution)/shard_map/ppermute | solution.py:448
  46.7 3.6 %collective-permute-start.4 = (f32[64,256]{1,0:T(8,128)S(1)}, f32[64,256]{1,0:T(8,128)S(1)}, u32[]{:S(2)}, u32[]{:S(2)}) collective-permute-start(f32[64,256]{1,0:T(8,128)S(1)} %add.10), channel_id=1, source_target_pairs={{0,48},{48,0},{16,32},{32,16},{1,49},{49,1},{17,33},{33,17},{2,50}... | collective-permute-start | bytes 196616 | tf_op jit(solution)/shard_map/ppermute | solution.py:449
  50.3 2.0 %collective-permute-done.4 = f32[64,256]{1,0:T(8,128)S(1)} collective-permute-done((f32[64,256]{1,0:T(8,128)S(1)}, f32[64,256]{1,0:T(8,128)S(1)}, u32[]{:S(2)}, u32[]{:S(2)}) %collective-permute-start.4) | collective-permute-done | bytes 65568 | tf_op jit(solution)/shard_map/ppermute | solution.py:449
  52.3 0.0 collective-permute-done.2.far_ref
  52.3 0.0 copy-start.4
  52.3 0.2 broadcast_in_dim.2
  52.5 0.0 copy-start
  52.6 0.0 copy-start.1
  52.6 0.0 copy-start.3
  52.6 30.9 %all_to_all.16 = f32[32,64,256]{2,1,0:T(8,128)S(1)} all-to-all(f32[32,64,256]{2,1,0:T(8,128)S(1)} %broadcast_in_dim.2), channel_id=1, replica_groups=mesh['dp'=2,'fsdp'=2,'zh'=4,'zl'=2,'y'=4,'xl'=2] {'dp','zl','y','xl'}, dimensions={0} | all-to-all | bytes 4194304 | tf_op jit(solution)/shard_map/all_to_all | solution.py:45
  83.4 0.0 copy-done.4
  83.5 0.0 copy-done
  83.5 0.0 copy-done.1
  83.5 0.0 copy-done.3
  83.5 2.1 %shard_map.69 = (f32[256,256]{1,0:T(8,128)S(1)}, f32[256,128]{1,0:T(8,128)S(1)}) custom-call(s32[1]{0:T(128)} %bitcast.1.replica_ref, f32[2048,256]{1,0:T(8,128)S(1)} %bitcast.8, f32[2048,128]{1,0:T(8,128)S(1)} %copy-done, bf16[2048,128]{1,0:T(8,128)(2,1)S(1)} %bitcast.13, f32[1024,128]{1,0:T(8,128)S(1)} %copy-done.3, ...), custom_call_target="tpu_custom_call" | custom-call | tf_op jit(solution)/shard_map/pallas_call | solution.py:173
  85.6 4.9 %collective-permute-start.5 = (f32[256,256]{1,0:T(8,128)S(1)}, f32[256,256]{1,0:T(8,128)S(1)}, u32[]{:S(2)}, u32[]{:S(2)}) collective-permute-start(f32[256,256]{1,0:T(8,128)S(1)} %get-tuple-element.23.gram_ref), channel_id=1, source_target_pairs={{0,64},{64,0},{1,65},{65,1},{2,66},{66,2},{3,67},{67,3},{4,68},{68... | collective-permute-start | bytes 786440 | tf_op jit(solution)/shard_map/ppermute | solution.py:40
  90.5 0.3 collective-permute-start.6
  90.8 1.1 collective-permute-done.6.other_product_ref
  91.9 0.0 collective-permute-done.5.other_gram_ref
  91.9 12.4 %shard_map.70 = (f32[256,256]{1,0:T(8,128)}, f32[256,128]{1,0:T(8,128)}, f32[256,128]{1,0:T(8,128)}, f32[64,1,256]{2,1,0:T(1,128)}) custom-call(f32[256,256]{1,0:T(8,128)S(1)} %get-tuple-element.23.gram_ref, f32[256,256]{1,0:T(8,128)S(1)} %collective-permute-done.5.other_gram_ref, f32[256,128]{1,0:T(8,128)S(1)} %get-tuple-element.24.product_ref, ...), custom_call_target="tpu_custom_call" | custom-call | tf_op jit(solution)/shard_map/pallas_call | solution.py:223
  104.3 8.3 %all-to-all-start.2 = ((f32[64,1,256]{2,1,0:T(1,128)}), f32[64,1,256]{2,1,0:T(1,128)S(1)}, u32[]{:S(2)}, u32[]{:S(2)}) async-start(f32[64,1,256]{2,1,0:T(1,128)} %get-tuple-element.25), calls=%async_computation.2 | async-start | bytes 131072 | tf_op jit(solution)/shard_map/all_to_all | solution.py:457
  112.5 0.0 copy-start.5
  112.5 0.0 copy-start.7
  112.6 4.8 %shard_map.72 = f32[2048,128]{1,0:T(8,128)} custom-call(s32[1]{0:T(128)} %bitcast.1.replica_ref, f32[2048,256]{1,0:T(8,128)S(1)} %bitcast.9, f32[256,128]{1,0:T(8,128)} %get-tuple-element.29.change_ref, f32[2048,128]{1,0:T(8,128)} %momentum_ref.5, bf16[2048,128]{1,0:T(8,128)(2,1)} %bitcast.12, f32[1024,128]{1,0:T(8,128)} %copy-done.2, f32[1024,128]{1,0:T(8,128)} %copy-done.4), custom_call_target="tpu_custom_call" | custom-call | flops 402653184 | bytes 4194304 | tf_op jit(solution)/shard_map/pallas_call | solution.py:264
  117.4 4.7 %all-to-all-done.2.squares_ref = f32[64,1,256]{2,1,0:T(1,128)S(1)} async-done(((f32[64,1,256]{2,1,0:T(1,128)}), f32[64,1,256]{2,1,0:T(1,128)S(1)}, u32[]{:S(2)}, u32[]{:S(2)}) %all-to-all-start.2) | async-done | bytes 65568 | tf_op jit(solution)/shard_map/all_to_all | solution.py:457
  122.1 0.0 copy-done.5
  122.1 0.0 copy-done.7
  122.1 4.0 %shard_map.71 = (f32[2048,128]{1,0:T(8,128)}, f32[128,128]{1,0:T(8,128)}) custom-call(s32[1]{0:T(128)S(6)} %mul.6.first_ref, f32[64,1,256]{2,1,0:T(1,128)S(1)} %all-to-all-done.2.squares_ref, f32[2048,256]{1,0:T(8,128)S(1)} %bitcast.10, f32[256,256]{1,0:T(8,128)S(1)} %copy-done.7, f32[256,128]{1,0:T(8,128)} %get-tuple-element.27.coefficients_ref, ...), custom_call_target="tpu_custom_call" | custom-call | tf_op jit(solution)/shard_map/pallas_call | solution.py:320
  (2 shorter events, 0.0 us)
Async XLA Ops:
  0.6 15.3 %copy-start.6 = (f32[128,128]{1,0:T(8,128)S(1)}, f32[128,128]{1,0:T(8,128)}, u32[]{:S(2)}) copy-start(f32[128,128]{1,0:T(8,128)} %own_ref.3) | copy-start | bytes 196612
  1.7 14.3 %collective-permute-start.1 = (f32[1024,128]{1,0:T(8,128)S(1)}, f32[1024,128]{1,0:T(8,128)S(1)}, u32[]{:S(2)}, u32[]{:S(2)}) collective-permute-start(f32[1024,128]{1,0:T(8,128)S(1)} %bitcast_convert_fusion), channel_id=1, source_target_pairs={{0,128},{128,0},{1,129},{129,1},{2,130},{130,2},{3,131},{131,3},{4... | collective-permute-start | bytes 1572872 | tf_op jit(solution)/shard_map/ppermute | solution.py:40
  5.3 2.1 %collective-permute-start = (f32[128,128]{1,0:T(8,128)}, f32[128,128]{1,0:T(8,128)S(1)}, u32[]{:S(2)}, u32[]{:S(2)}) collective-permute-start(f32[128,128]{1,0:T(8,128)} %own_ref.3), channel_id=1, source_target_pairs={{0,64},{64,0},{1,65},{65,1},{2,66},{66,2},{3,67},{67,3},{4,68},{68... | collective-permute-start | bytes 196616 | tf_op jit(solution)/shard_map/ppermute | solution.py:40
  15.9 22.5 %copy-start.2 = (f32[1024,128]{1,0:T(8,128)}, f32[1024,128]{1,0:T(8,128)S(1)}, u32[]{:S(2)}) copy-start(f32[1024,128]{1,0:T(8,128)S(1)} %collective-permute-done.1.near_ref) | copy-start | bytes 1572868
  38.5 13.8 %collective-permute-start.2 = (f32[1024,128]{1,0:T(8,128)S(1)}, f32[1024,128]{1,0:T(8,128)S(1)}, u32[]{:S(2)}, u32[]{:S(2)}) collective-permute-start(f32[1024,128]{1,0:T(8,128)S(1)} %get-tuple-element.19), channel_id=1, source_target_pairs={{0,128},{128,0},{1,129},{129,1},{2,130},{130,2},{3,131},{131,3},{4... | collective-permute-start | bytes 1572872 | tf_op jit(solution)/shard_map/ppermute | solution.py:40
  41.0 5.6 %collective-permute-start.3 = (f32[64,256]{1,0:T(8,128)S(1)}, f32[64,256]{1,0:T(8,128)S(1)}, u32[]{:S(2)}, u32[]{:S(2)}) collective-permute-start(f32[64,256]{1,0:T(8,128)S(1)} %reduce_sum.9), channel_id=1, source_target_pairs={{0,16},{16,0},{32,48},{48,32},{1,17},{17,1},{33,49},{49,33},{2,18}... | collective-permute-start | bytes 196616 | tf_op jit(solution)/shard_map/ppermute | solution.py:448
  46.7 5.6 %collective-permute-start.4 = (f32[64,256]{1,0:T(8,128)S(1)}, f32[64,256]{1,0:T(8,128)S(1)}, u32[]{:S(2)}, u32[]{:S(2)}) collective-permute-start(f32[64,256]{1,0:T(8,128)S(1)} %add.10), channel_id=1, source_target_pairs={{0,48},{48,0},{16,32},{32,16},{1,49},{49,1},{17,33},{33,17},{2,50}... | collective-permute-start | bytes 196616 | tf_op jit(solution)/shard_map/ppermute | solution.py:449
  52.3 31.1 %copy-start.4 = (f32[1024,128]{1,0:T(8,128)}, f32[1024,128]{1,0:T(8,128)S(1)}, u32[]{:S(2)}) copy-start(f32[1024,128]{1,0:T(8,128)S(1)} %collective-permute-done.2.far_ref) | copy-start | bytes 1572868
  52.5 30.9 %copy-start = (f32[2048,128]{1,0:T(8,128)S(1)}, f32[2048,128]{1,0:T(8,128)}, u32[]{:S(2)}) copy-start(f32[2048,128]{1,0:T(8,128)} %momentum_ref.5) | copy-start | bytes 3145732
  52.6 30.9 %copy-start.1 = (bf16[1,1,2048,128]{3,2,1,0:T(8,128)(2,1)S(1)}, bf16[1,1,2048,128]{3,2,1,0:T(8,128)(2,1)}, u32[]{:S(2)}) copy-start(bf16[1,1,2048,128]{3,2,1,0:T(8,128)(2,1)} %param.7) | copy-start | bytes 1572868
  52.6 30.9 %copy-start.3 = (f32[1024,128]{1,0:T(8,128)S(1)}, f32[1024,128]{1,0:T(8,128)}, u32[]{:S(2)}) copy-start(f32[1024,128]{1,0:T(8,128)} %copy-done.2) | copy-start | bytes 1572868
  85.6 6.3 %collective-permute-start.5 = (f32[256,256]{1,0:T(8,128)S(1)}, f32[256,256]{1,0:T(8,128)S(1)}, u32[]{:S(2)}, u32[]{:S(2)}) collective-permute-start(f32[256,256]{1,0:T(8,128)S(1)} %get-tuple-element.23.gram_ref), channel_id=1, source_target_pairs={{0,64},{64,0},{1,65},{65,1},{2,66},{66,2},{3,67},{67,3},{4,68},{68... | collective-permute-start | bytes 786440 | tf_op jit(solution)/shard_map/ppermute | solution.py:40
  90.5 1.3 %collective-permute-start.6 = (f32[256,128]{1,0:T(8,128)S(1)}, f32[256,128]{1,0:T(8,128)S(1)}, u32[]{:S(2)}, u32[]{:S(2)}) collective-permute-start(f32[256,128]{1,0:T(8,128)S(1)} %get-tuple-element.24.product_ref), channel_id=1, source_target_pairs={{0,64},{64,0},{1,65},{65,1},{2,66},{66,2},{3,67},{67,3},{4,68},{68... | collective-permute-start | bytes 393224 | tf_op jit(solution)/shard_map/ppermute | solution.py:40
  104.3 17.9 %all-to-all-start.2 = ((f32[64,1,256]{2,1,0:T(1,128)}), f32[64,1,256]{2,1,0:T(1,128)S(1)}, u32[]{:S(2)}, u32[]{:S(2)}) async-start(f32[64,1,256]{2,1,0:T(1,128)} %get-tuple-element.25), calls=%async_computation.2 | async-start | bytes 131072 | tf_op jit(solution)/shard_map/all_to_all | solution.py:457
  112.5 9.6 %copy-start.5 = (f32[2048,128]{1,0:T(8,128)S(1)}, f32[2048,128]{1,0:T(8,128)}, u32[]{:S(2)}) copy-start(f32[2048,128]{1,0:T(8,128)} %weight_ref.1) | copy-start | bytes 3145732
  112.5 9.6 %copy-start.7 = (f32[256,256]{1,0:T(8,128)S(1)}, f32[256,256]{1,0:T(8,128)}, u32[]{:S(2)}) copy-start(f32[256,256]{1,0:T(8,128)} %get-tuple-element.26.inverse_ref) | copy-start | bytes 786436

commit v3 on v2

--- a/solution.py
+++ b/solution.py
@@ -136,9 +136,9 @@
 
     left_high, left_low = split(left)
     right_high, right_low = split(right)
-    return product(left_high, right_high) + (
-        product(left_high, right_low) + product(left_low, right_high)
-    )
+    width = right.shape[1]
+    high = product(left_high, jnp.concatenate([right_high, right_low], axis=1))
+    return high[:, :width] + (high[:, width:] + product(left_low, right_high))
 
 
 def moments_kernel(
@@ -163,7 +163,9 @@
             b1, b2 = split(total)
             one_side += product(a1, a2) + product(a1, a3)
             gram += product(a1, a1) + product(a2, a2)
-            moved += product(a1, b1) + (product(a1, b2) + product(a2, b1))
+            high = product(a1, jnp.concatenate([b1, b2], axis=1))
+            width = b1.shape[1]
+            moved += high[:, :width] + (high[:, width:] + product(a2, b1))
     gram_ref[...] = gram + (one_side + one_side.T)
     product_ref[...] = moved
 
@@ -316,7 +318,7 @@
 
 def new_weight(first, squares, sketch, inverse, coefficients, weight, share):
     rows, columns = weight.shape
-    steps = 8
+    steps = 4
     return pl.pallas_call(
         weight_kernel,
         compiler_params=pltpu.CompilerParams(vmem_limit_bytes=KERNEL_VMEM),

time: 127 us -> 126 us (level)
  no operation moved by 1% of the time
where the time goes in v3:
time: 126 us
  blocking collectives  52.2 us (41%)
  starting transfers between devices  27.2 us (22%)
  Pallas kernels  26.4 us (21%)
  waiting for transfers between devices  17.4 us (14%)
    all_to_all x1, blocking collectives, sent_to_all(): lax.all_to_all(jnp.broadcast_to(value[None], (length, *value.shape)), axi...  30.9 us
    all_to_all x1, blocking collectives, sum_at_owner(): return lax.all_to_all(pieces, axis, 0, 0, tiled=True).sum(axis=0)  21.3 us
    pallas_call x1, Pallas kernels, small_part(): pl.pallas_call(coefficients_kernel, compiler_params=pltpu.CompilerParams(...  12.4 us
    ppermute x5, starting transfers between devices, swapped(): return lax.ppermute(value, axis, [(0, 1), (1, 0)])  12.4 us
    all_to_all x1, starting transfers between devices, step(): squares = lax.all_to_all(squares, TENSOR, 0, 0, tiled=True)  8.27 us
    ppermute x5, waiting for transfers between devices, swapped(): return lax.ppermute(value, axis, [(0, 1), (1, 0)])  7.88 us
    all_to_all x1, waiting for transfers between devices, step(): squares = lax.all_to_all(squares, TENSOR, 0, 0, tiled=True)  4.88 us
    pallas_call x1, Pallas kernels, new_momentum(): pl.pallas_call(momentum_kernel, compiler_params=pltpu.CompilerParams(vmem...  4.7 us
  transfers between devices with their start and end apart: 8, of which 6 were waited for; matrix products, arithmetic and copies ran while one was open for 0% of the time, Pallas kernels for 6%

profile of v3, /device:TPU:1, one launch (start us, length us, event | category | flops | bytes accessed | tf_op | source)
XLA Modules:
  0.0 125.6 jit_solution(1469878335843982517)
XLA Ops:
  0.6 0.0 copy-start.6
  0.6 1.0 bitcast_convert_fusion
  1.7 3.6 %collective-permute-start.1 = (f32[1024,128]{1,0:T(8,128)S(1)}, f32[1024,128]{1,0:T(8,128)S(1)}, u32[]{:S(2)}, u32[]{:S(2)}) collective-permute-start(f32[1024,128]{1,0:T(8,128)S(1)} %bitcast_convert_fusion), channel_id=1, source_target_pairs={{0,128},{128,0},{1,129},{129,1},{2,130},{130,2},{3,131},{131,3},{4... | collective-permute-start | bytes 1572872 | tf_op jit(solution)/shard_map/ppermute | solution.py:40
  5.3 1.0 collective-permute-start
  6.3 0.1 pad_add_fusion.place_ref
  6.4 1.0 collective-permute-done.other_ref
  7.4 2.8 %shard_map.67 = (f32[1024,256]{1,0:T(8,128)S(1)}, f32[1024,128]{1,0:T(8,128)S(1)}) custom-call(s32[2]{0:T(128)S(1)} %pad_add_fusion.place_ref, f32[2048,128]{1,0:T(8,128)} %momentum_ref.5, bf16[2048,128]{1,0:T(8,128)(2,1)} %bitcast.11, f32[128,128]{1,0:T(8,128)} %own_ref.3, f32[128,128]{1,0:T(8,128)S(1)} %collective-permute-done.other_ref), custom_call_target="tpu_custom_call" | custom-call | flops 402653184 | bytes 2621440 | tf_op jit(solution)/shard_map/pallas_call | solution.py:403
  10.2 5.8 %collective-permute-done.1.near_ref = f32[1024,128]{1,0:T(8,128)S(1)} collective-permute-done((f32[1024,128]{1,0:T(8,128)S(1)}, f32[1024,128]{1,0:T(8,128)S(1)}, u32[]{:S(2)}, u32[]{:S(2)}) %collective-permute-start.1) | collective-permute-done | bytes 524320 | tf_op jit(solution)/shard_map/ppermute | solution.py:40
  15.9 0.0 copy-start.2
  15.9 0.0 copy-done.6
  15.9 1.1 shard_map.68
  17.1 21.3 %all_to_all.15 = f32[16,64,256]{2,1,0:T(8,128)S(1)} all-to-all(f32[16,64,256]{2,1,0:T(8,128)S(1)} %bitcast.14), channel_id=1, replica_groups=mesh['dp'=2,'fsdp'=2,'zh'=4,'zl'=2,'y'=4,'xl'=2] {'zl','y','xl'}, dimensions={0} | all-to-all | bytes 2097152 | tf_op jit(solution)/shard_map/all_to_all | solution.py:53
  38.4 0.0 copy-done.2
  38.4 0.1 reduce_sum.9
  38.5 2.5 %collective-permute-start.2 = (f32[1024,128]{1,0:T(8,128)S(1)}, f32[1024,128]{1,0:T(8,128)S(1)}, u32[]{:S(2)}, u32[]{:S(2)}) collective-permute-start(f32[1024,128]{1,0:T(8,128)S(1)} %get-tuple-element.19), channel_id=1, source_target_pairs={{0,128},{128,0},{1,129},{129,1},{2,130},{130,2},{3,131},{131,3},{4... | collective-permute-start | bytes 1572872 | tf_op jit(solution)/shard_map/ppermute | solution.py:40
  41.0 3.0 %collective-permute-start.3 = (f32[64,256]{1,0:T(8,128)S(1)}, f32[64,256]{1,0:T(8,128)S(1)}, u32[]{:S(2)}, u32[]{:S(2)}) collective-permute-start(f32[64,256]{1,0:T(8,128)S(1)} %reduce_sum.9), channel_id=1, source_target_pairs={{0,16},{16,0},{32,48},{48,32},{1,17},{17,1},{33,49},{49,33},{2,18}... | collective-permute-start | bytes 196616 | tf_op jit(solution)/shard_map/ppermute | solution.py:450
  44.0 2.6 %collective-permute-done.3 = f32[64,256]{1,0:T(8,128)S(1)} collective-permute-done((f32[64,256]{1,0:T(8,128)S(1)}, f32[64,256]{1,0:T(8,128)S(1)}, u32[]{:S(2)}, u32[]{:S(2)}) %collective-permute-start.3) | collective-permute-done | bytes 65568 | tf_op jit(solution)/shard_map/ppermute | solution.py:450
  46.7 3.6 %collective-permute-start.4 = (f32[64,256]{1,0:T(8,128)S(1)}, f32[64,256]{1,0:T(8,128)S(1)}, u32[]{:S(2)}, u32[]{:S(2)}) collective-permute-start(f32[64,256]{1,0:T(8,128)S(1)} %add.10), channel_id=1, source_target_pairs={{0,48},{48,0},{16,32},{32,16},{1,49},{49,1},{17,33},{33,17},{2,50}... | collective-permute-start | bytes 196616 | tf_op jit(solution)/shard_map/ppermute | solution.py:451
  50.3 2.0 %collective-permute-done.4 = f32[64,256]{1,0:T(8,128)S(1)} collective-permute-done((f32[64,256]{1,0:T(8,128)S(1)}, f32[64,256]{1,0:T(8,128)S(1)}, u32[]{:S(2)}, u32[]{:S(2)}) %collective-permute-start.4) | collective-permute-done | bytes 65568 | tf_op jit(solution)/shard_map/ppermute | solution.py:451
  52.3 0.0 collective-permute-done.2.far_ref
  52.3 0.0 copy-start.4
  52.3 0.2 broadcast_in_dim.2
  52.5 0.0 copy-start
  52.6 0.0 copy-start.1
  52.6 0.0 copy-start.3
  52.6 30.9 %all_to_all.16 = f32[32,64,256]{2,1,0:T(8,128)S(1)} all-to-all(f32[32,64,256]{2,1,0:T(8,128)S(1)} %broadcast_in_dim.2), channel_id=1, replica_groups=mesh['dp'=2,'fsdp'=2,'zh'=4,'zl'=2,'y'=4,'xl'=2] {'dp','zl','y','xl'}, dimensions={0} | all-to-all | bytes 4194304 | tf_op jit(solution)/shard_map/all_to_all | solution.py:45
  83.4 0.0 copy-done.4
  83.5 0.0 copy-done
  83.5 0.0 copy-done.1
  83.5 0.0 copy-done.3
  83.5 1.9 %shard_map.69 = (f32[256,256]{1,0:T(8,128)S(1)}, f32[256,128]{1,0:T(8,128)S(1)}) custom-call(s32[1]{0:T(128)} %bitcast.1.replica_ref, f32[2048,256]{1,0:T(8,128)S(1)} %bitcast.8, f32[2048,128]{1,0:T(8,128)S(1)} %copy-done, bf16[2048,128]{1,0:T(8,128)(2,1)S(1)} %bitcast.13, f32[1024,128]{1,0:T(8,128)S(1)} %copy-done.3, ...), custom_call_target="tpu_custom_call" | custom-call | tf_op jit(solution)/shard_map/pallas_call | solution.py:175
  85.3 4.9 %collective-permute-start.5 = (f32[256,256]{1,0:T(8,128)S(1)}, f32[256,256]{1,0:T(8,128)S(1)}, u32[]{:S(2)}, u32[]{:S(2)}) collective-permute-start(f32[256,256]{1,0:T(8,128)S(1)} %get-tuple-element.23.gram_ref), channel_id=1, source_target_pairs={{0,64},{64,0},{1,65},{65,1},{2,66},{66,2},{3,67},{67,3},{4,68},{68... | collective-permute-start | bytes 786440 | tf_op jit(solution)/shard_map/ppermute | solution.py:40
  90.3 0.3 collective-permute-start.6
  90.5 1.1 collective-permute-done.6.other_product_ref
  91.6 0.0 collective-permute-done.5.other_gram_ref
  91.6 12.4 %shard_map.70 = (f32[256,256]{1,0:T(8,128)}, f32[256,128]{1,0:T(8,128)}, f32[256,128]{1,0:T(8,128)}, f32[64,1,256]{2,1,0:T(1,128)}) custom-call(f32[256,256]{1,0:T(8,128)S(1)} %get-tuple-element.23.gram_ref, f32[256,256]{1,0:T(8,128)S(1)} %collective-permute-done.5.other_gram_ref, f32[256,128]{1,0:T(8,128)S(1)} %get-tuple-element.24.product_ref, ...), custom_call_target="tpu_custom_call" | custom-call | tf_op jit(solution)/shard_map/pallas_call | solution.py:225
  104.0 8.3 %all-to-all-start.2 = ((f32[64,1,256]{2,1,0:T(1,128)}), f32[64,1,256]{2,1,0:T(1,128)S(1)}, u32[]{:S(2)}, u32[]{:S(2)}) async-start(f32[64,1,256]{2,1,0:T(1,128)} %get-tuple-element.25), calls=%async_computation.2 | async-start | bytes 131072 | tf_op jit(solution)/shard_map/all_to_all | solution.py:459
  112.3 0.0 copy-start.5
  112.3 0.0 copy-start.7
  112.3 4.7 %shard_map.72 = f32[2048,128]{1,0:T(8,128)} custom-call(s32[1]{0:T(128)} %bitcast.1.replica_ref, f32[2048,256]{1,0:T(8,128)S(1)} %bitcast.9, f32[256,128]{1,0:T(8,128)} %get-tuple-element.29.change_ref, f32[2048,128]{1,0:T(8,128)} %momentum_ref.5, bf16[2048,128]{1,0:T(8,128)(2,1)} %bitcast.12, f32[1024,128]{1,0:T(8,128)} %copy-done.2, f32[1024,128]{1,0:T(8,128)} %copy-done.4), custom_call_target="tpu_custom_call" | custom-call | flops 402653184 | bytes 4194304 | tf_op jit(solution)/shard_map/pallas_call | solution.py:266
  117.0 4.9 %all-to-all-done.2.squares_ref = f32[64,1,256]{2,1,0:T(1,128)S(1)} async-done(((f32[64,1,256]{2,1,0:T(1,128)}), f32[64,1,256]{2,1,0:T(1,128)S(1)}, u32[]{:S(2)}, u32[]{:S(2)}) %all-to-all-start.2) | async-done | bytes 65568 | tf_op jit(solution)/shard_map/all_to_all | solution.py:459
  121.9 0.0 copy-done.5
  121.9 0.0 copy-done.7
  121.9 3.6 %shard_map.71 = (f32[2048,128]{1,0:T(8,128)}, f32[128,128]{1,0:T(8,128)}) custom-call(s32[1]{0:T(128)S(6)} %mul.6.first_ref, f32[64,1,256]{2,1,0:T(1,128)S(1)} %all-to-all-done.2.squares_ref, f32[2048,256]{1,0:T(8,128)S(1)} %bitcast.10, f32[256,256]{1,0:T(8,128)S(1)} %copy-done.7, f32[256,128]{1,0:T(8,128)} %get-tuple-element.27.coefficients_ref, ...), custom_call_target="tpu_custom_call" | custom-call | tf_op jit(solution)/shard_map/pallas_call | solution.py:322
  (2 shorter events, 0.0 us)
Async XLA Ops:
  0.6 15.3 %copy-start.6 = (f32[128,128]{1,0:T(8,128)S(1)}, f32[128,128]{1,0:T(8,128)}, u32[]{:S(2)}) copy-start(f32[128,128]{1,0:T(8,128)} %own_ref.3) | copy-start | bytes 196612
  1.7 14.3 %collective-permute-start.1 = (f32[1024,128]{1,0:T(8,128)S(1)}, f32[1024,128]{1,0:T(8,128)S(1)}, u32[]{:S(2)}, u32[]{:S(2)}) collective-permute-start(f32[1024,128]{1,0:T(8,128)S(1)} %bitcast_convert_fusion), channel_id=1, source_target_pairs={{0,128},{128,0},{1,129},{129,1},{2,130},{130,2},{3,131},{131,3},{4... | collective-permute-start | bytes 1572872 | tf_op jit(solution)/shard_map/ppermute | solution.py:40
  5.3 2.1 %collective-permute-start = (f32[128,128]{1,0:T(8,128)}, f32[128,128]{1,0:T(8,128)S(1)}, u32[]{:S(2)}, u32[]{:S(2)}) collective-permute-start(f32[128,128]{1,0:T(8,128)} %own_ref.3), channel_id=1, source_target_pairs={{0,64},{64,0},{1,65},{65,1},{2,66},{66,2},{3,67},{67,3},{4,68},{68... | collective-permute-start | bytes 196616 | tf_op jit(solution)/shard_map/ppermute | solution.py:40
  15.9 22.5 %copy-start.2 = (f32[1024,128]{1,0:T(8,128)}, f32[1024,128]{1,0:T(8,128)S(1)}, u32[]{:S(2)}) copy-start(f32[1024,128]{1,0:T(8,128)S(1)} %collective-permute-done.1.near_ref) | copy-start | bytes 1572868
  38.5 13.8 %collective-permute-start.2 = (f32[1024,128]{1,0:T(8,128)S(1)}, f32[1024,128]{1,0:T(8,128)S(1)}, u32[]{:S(2)}, u32[]{:S(2)}) collective-permute-start(f32[1024,128]{1,0:T(8,128)S(1)} %get-tuple-element.19), channel_id=1, source_target_pairs={{0,128},{128,0},{1,129},{129,1},{2,130},{130,2},{3,131},{131,3},{4... | collective-permute-start | bytes 1572872 | tf_op jit(solution)/shard_map/ppermute | solution.py:40
  41.0 5.6 %collective-permute-start.3 = (f32[64,256]{1,0:T(8,128)S(1)}, f32[64,256]{1,0:T(8,128)S(1)}, u32[]{:S(2)}, u32[]{:S(2)}) collective-permute-start(f32[64,256]{1,0:T(8,128)S(1)} %reduce_sum.9), channel_id=1, source_target_pairs={{0,16},{16,0},{32,48},{48,32},{1,17},{17,1},{33,49},{49,33},{2,18}... | collective-permute-start | bytes 196616 | tf_op jit(solution)/shard_map/ppermute | solution.py:450
  46.7 5.6 %collective-permute-start.4 = (f32[64,256]{1,0:T(8,128)S(1)}, f32[64,256]{1,0:T(8,128)S(1)}, u32[]{:S(2)}, u32[]{:S(2)}) collective-permute-start(f32[64,256]{1,0:T(8,128)S(1)} %add.10), channel_id=1, source_target_pairs={{0,48},{48,0},{16,32},{32,16},{1,49},{49,1},{17,33},{33,17},{2,50}... | collective-permute-start | bytes 196616 | tf_op jit(solution)/shard_map/ppermute | solution.py:451
  52.3 31.1 %copy-start.4 = (f32[1024,128]{1,0:T(8,128)}, f32[1024,128]{1,0:T(8,128)S(1)}, u32[]{:S(2)}) copy-start(f32[1024,128]{1,0:T(8,128)S(1)} %collective-permute-done.2.far_ref) | copy-start | bytes 1572868
  52.5 30.9 %copy-start = (f32[2048,128]{1,0:T(8,128)S(1)}, f32[2048,128]{1,0:T(8,128)}, u32[]{:S(2)}) copy-start(f32[2048,128]{1,0:T(8,128)} %momentum_ref.5) | copy-start | bytes 3145732
  52.6 30.9 %copy-start.1 = (bf16[1,1,2048,128]{3,2,1,0:T(8,128)(2,1)S(1)}, bf16[1,1,2048,128]{3,2,1,0:T(8,128)(2,1)}, u32[]{:S(2)}) copy-start(bf16[1,1,2048,128]{3,2,1,0:T(8,128)(2,1)} %param.7) | copy-start | bytes 1572868
  52.6 30.9 %copy-start.3 = (f32[1024,128]{1,0:T(8,128)S(1)}, f32[1024,128]{1,0:T(8,128)}, u32[]{:S(2)}) copy-start(f32[1024,128]{1,0:T(8,128)} %copy-done.2) | copy-start | bytes 1572868
  85.3 6.3 %collective-permute-start.5 = (f32[256,256]{1,0:T(8,128)S(1)}, f32[256,256]{1,0:T(8,128)S(1)}, u32[]{:S(2)}, u32[]{:S(2)}) collective-permute-start(f32[256,256]{1,0:T(8,128)S(1)} %get-tuple-element.23.gram_ref), channel_id=1, source_target_pairs={{0,64},{64,0},{1,65},{65,1},{2,66},{66,2},{3,67},{67,3},{4,68},{68... | collective-permute-start | bytes 786440 | tf_op jit(solution)/shard_map/ppermute | solution.py:40
  90.3 1.3 %collective-permute-start.6 = (f32[256,128]{1,0:T(8,128)S(1)}, f32[256,128]{1,0:T(8,128)S(1)}, u32[]{:S(2)}, u32[]{:S(2)}) collective-permute-start(f32[256,128]{1,0:T(8,128)S(1)} %get-tuple-element.24.product_ref), channel_id=1, source_target_pairs={{0,64},{64,0},{1,65},{65,1},{2,66},{66,2},{3,67},{67,3},{4,68},{68... | collective-permute-start | bytes 393224 | tf_op jit(solution)/shard_map/ppermute | solution.py:40
  104.0 17.9 %all-to-all-start.2 = ((f32[64,1,256]{2,1,0:T(1,128)}), f32[64,1,256]{2,1,0:T(1,128)S(1)}, u32[]{:S(2)}, u32[]{:S(2)}) async-start(f32[64,1,256]{2,1,0:T(1,128)} %get-tuple-element.25), calls=%async_computation.2 | async-start | bytes 131072 | tf_op jit(solution)/shard_map/all_to_all | solution.py:459
  112.3 9.6 %copy-start.5 = (f32[2048,128]{1,0:T(8,128)S(1)}, f32[2048,128]{1,0:T(8,128)}, u32[]{:S(2)}) copy-start(f32[2048,128]{1,0:T(8,128)} %weight_ref.1) | copy-start | bytes 3145732
  112.3 9.6 %copy-start.7 = (f32[256,256]{1,0:T(8,128)S(1)}, f32[256,256]{1,0:T(8,128)}, u32[]{:S(2)}) copy-start(f32[256,256]{1,0:T(8,128)} %get-tuple-element.26.inverse_ref) | copy-start | bytes 786436
